TPU v7x, 128 devices: a whole 4x4x4 slice. The times are simulated.
128 devices in a mesh: gx: 4 (over y), gy: 32 (over x, z, core).
Axes of the slice: x: 4, y: 4, z: 4, core: 2. Of those that a mesh axis runs over, the one named last changes fastest.
Arguments:
- slave_coords: float32 [3, 8388608], P(None, ('gx', 'gy')), may hold values from -6 to 6
- slave_weight: float32 [8388608], P(('gx', 'gy')), may hold values from 0.5 to 2
- master_ctrl: float32 [3, 8388608], P(None, ('gx', 'gy')), may hold values from -6 to 6
- master_wt: float32 [8388608], P(('gx', 'gy')), may hold values from 0.5 to 2
- pair_slave: int32 [81920], P(('gx', 'gy')), may hold values from 0 to 511
- pair_master: int32 [81920], P(('gx', 'gy')), may hold values from 0 to 255
- pair_count: int32 [16384], P(('gx', 'gy')), may hold values from 0 to 5, as said below
Outputs:
- slave_force: float32 [3, 8388608], P(None, ('gx', 'gy'))
- master_force: float32 [3, 8388608], P(None, ('gx', 'gy'))
Inputs may be any that keep to these rules, and one draw needn't show every extreme that they name: `pair_count`: entry s * 128 + o counts the live slots from device s to owner o; in every draw some owner gets 5 live slots from every device. `pair_slave`: entries of slots that are not live are block numbers too and change nothing.
All inputs are finite; a program needn't handle non-finite values.
Results may differ from a plain program's by a relative error of at most 0.0003.
Values sent between devices are 32-bit elements; how exact they have to be, the bound alone decides.
No kernel may reach another device: no remote copies, remote signals or barrier semaphores. Data moves between devices by JAX's collectives and lax.ppermute only.
A program may use at most 64 MiB of HBM per device.

v0:
```python
import math

import jax
import jax.numpy as jnp
from jax import lax
from jax.sharding import PartitionSpec as P

QP = 128
CAP = 5
SB_DEV = 512
MB_DEV = 256
MP = 256


inverse_width = 1.0 / 3.0
force_gain = 0.01


def bezier_table():
    params = (jnp.arange(4, dtype=jnp.float32) + 0.5) / 4.0
    powers = jnp.arange(4, dtype=jnp.float32)
    binomial = jnp.array([1.0, 3.0, 3.0, 1.0], dtype=jnp.float32)
    bernstein = (
        binomial[None, :]
        * params[:, None] ** powers[None, :]
        * (1.0 - params[:, None]) ** (3.0 - powers[None, :])
    )
    return (bernstein[:, None, :, None] * bernstein[None, :, None, :]).reshape(16, 16)


def sample_blocks(blocks):
    block_count = blocks.shape[1]
    patch_count = blocks.shape[2] // 16
    basis_table = bezier_table()
    patch_grid = blocks.reshape(4, block_count, patch_count, 16)
    weights = patch_grid[3]
    numerator = jnp.einsum(
        "jk,cnpk->cnpj",
        basis_table,
        patch_grid[:3] * weights[None],
        precision=lax.Precision.HIGHEST,
    )
    denominator = jnp.einsum("jk,npk->npj", basis_table, weights, precision=lax.Precision.HIGHEST)
    samples = (numerator / denominator[None]).reshape(3, block_count, patch_count * 16)
    spread = basis_table[None, None] * weights[:, :, None, :] / denominator[..., None]
    return (samples, spread)


def tile_forces(points, weights, blocks):
    samples, spread = sample_blocks(blocks)
    block_count = blocks.shape[1]
    patch_count = blocks.shape[2] // 16
    differ = points[:, :, :, None] - samples[:, :, None, :]
    distance = jnp.sum(differ * differ, axis=0)
    kernel = weights[:, :, None] * jnp.exp(-distance * inverse_width) * force_gain
    weighted = kernel[None] * differ
    slave_term = jnp.sum(weighted, axis=3)
    sample_term = -jnp.sum(weighted, axis=2)
    sample_grid = sample_term.reshape(3, block_count, patch_count, 16)
    master_term = jnp.sum(spread[None] * sample_grid[..., None], axis=3)
    return (slave_term, master_term.reshape(3, block_count, patch_count * 16))


def all_tiles(points, weights, blocks):
    slot_count = weights.shape[0]
    group_size = math.gcd(slot_count, 32)

    def one_group(position, carried):
        slave_slots, master_slots = carried
        first_slot = position * group_size
        slave_term, master_term = tile_forces(
            lax.dynamic_slice_in_dim(points, first_slot, group_size, 1),
            lax.dynamic_slice_in_dim(weights, first_slot, group_size, 0),
            lax.dynamic_slice_in_dim(blocks, first_slot, group_size, 1),
        )
        slave_slots = lax.dynamic_update_slice_in_dim(slave_slots, slave_term, first_slot, 1)
        master_slots = lax.dynamic_update_slice_in_dim(master_slots, master_term, first_slot, 1)
        return (slave_slots, master_slots)

    initial = (
        jnp.zeros((3, slot_count, points.shape[2]), jnp.float32),
        jnp.zeros((3, slot_count, blocks.shape[2]), jnp.float32),
    )
    return lax.fori_loop(0, slot_count // group_size, one_group, initial)


def collect(slot_forces, block_ids, block_total):
    selector = (jnp.arange(block_total, dtype=jnp.int32)[:, None] == block_ids[None, :]).astype(
        jnp.float32
    )
    return jnp.einsum("bs,csq->cbq", selector, slot_forces, precision=lax.Precision.HIGHEST)


def relay_out(payload, outer_count, inner_count):
    components, slot_count, columns = payload.shape
    per_owner = slot_count // (outer_count * inner_count)
    moved = lax.all_to_all(
        payload.reshape(components, outer_count * inner_count, per_owner, columns),
        ("gx", "gy"),
        split_axis=1,
        concat_axis=1,
        tiled=True,
    )
    return moved.reshape(components, slot_count, columns)


def relay_back(payload, outer_count, inner_count):
    components, slot_count, columns = payload.shape
    per_owner = slot_count // (outer_count * inner_count)
    moved = lax.all_to_all(
        payload.reshape(components, outer_count * inner_count, per_owner, columns),
        ("gx", "gy"),
        split_axis=1,
        concat_axis=1,
        tiled=True,
    )
    return moved.reshape(components, slot_count, columns)


def body(slave_coords, slave_weight, master_ctrl, master_wt, pair_slave, pair_master, pair_count):
    outer_count = lax.axis_size("gx")
    inner_count = lax.axis_size("gy")
    owners = outer_count * inner_count
    slot_count = pair_slave.shape[0]
    slot_index = jnp.arange(slot_count, dtype=jnp.int32)
    live_mask = (slot_index % CAP < jnp.repeat(pair_count, CAP)).astype(jnp.float32)
    incoming = lax.all_to_all(
        pair_master.reshape(owners, CAP), ("gx", "gy"), split_axis=0, concat_axis=0, tiled=True
    ).reshape(slot_count)
    slave_grid = slave_coords.reshape(3, SB_DEV, QP)
    own_blocks = jnp.concatenate([master_ctrl, master_wt[None, :]], axis=0).reshape(4, MB_DEV, MP)
    tile_points = jnp.take(slave_grid, pair_slave, axis=1)
    tile_weights = (
        jnp.take(slave_weight.reshape(SB_DEV, QP), pair_slave, axis=0) * live_mask[:, None]
    )
    fetched = relay_out(jnp.take(own_blocks, incoming, axis=1), outer_count, inner_count)
    slave_slots, master_slots = all_tiles(tile_points, tile_weights, fetched)
    slave_total = collect(slave_slots, pair_slave, SB_DEV)
    master_total = collect(relay_back(master_slots, outer_count, inner_count), incoming, MB_DEV)
    return (slave_total.reshape(3, SB_DEV * QP), master_total.reshape(3, MB_DEV * MP))


def solution(mesh):
    placed = (
        P(None, ("gx", "gy")),
        P(("gx", "gy")),
        P(None, ("gx", "gy")),
        P(("gx", "gy")),
        P(("gx", "gy")),
        P(("gx", "gy")),
        P(("gx", "gy")),
    )
    return jax.shard_map(
        body,
        mesh=mesh,
        in_specs=placed,
        out_specs=(P(None, ("gx", "gy")), P(None, ("gx", "gy"))),
        check_vma=False,
    )
```

profile of v0, /device:TPU:0, one launch (start us, length us, event | category | flops | bytes accessed | tf_op | source)
XLA Modules:
  0.0 410.1 jit_solution(17515691493822358516)
XLA Ops:
  2.2 11.2 %all-to-all-start = ((s32[128,1,5]{2,1,0:T(1,128)}), s32[128,1,5]{2,1,0:T(1,128)S(1)}, u32[]{:S(2)}, u32[]{:S(2)}) async-start(s32[128,1,5]{2,1,0:T(1,128)} %bitcast.3), calls=%async_computation | async-start | bytes 131072 | tf_op jit(solution)/shard_map/all_to_all | solution.py:127
  15.2 7.7 %all-to-all-done = s32[128,1,5]{2,1,0:T(1,128)S(1)} async-done(((s32[128,1,5]{2,1,0:T(1,128)}), s32[128,1,5]{2,1,0:T(1,128)S(1)}, u32[]{:S(2)}, u32[]{:S(2)}) %all-to-all-start) | async-done | bytes 2592 | tf_op jit(solution)/shard_map/all_to_all | solution.py:127
  24.5 4.1 %gather_fusion.2 = f32[640,4,256]{2,1,0:T(4,128)} fusion(f32[4,256,256]{2,0,1:T(4,128)S(1)} %pad_maximum_fusion, s32[1024]{0:T(1024)S(1)} %pad_clamp_fusion), kind=kCustom, calls=%fused_computation.2 | custom fusion | bytes 5245440 | tf_op jit(solution)/shard_map/jit(_take)/gather | solution.py:136
  28.6 4.7 %broadcast_select_fusion = f32[4,128,5,256]{3,0,2,1:T(4,128)} fusion(f32[4,128,5,256]{3,0,2,1:T(4,128)} %bitcast.74, pred[128,5]{1,0:T(8,128)(4,1)S(1)} %compare_and_fusion), kind=kLoop, calls=%fused_computation.29 | loop fusion | flops 655360 | bytes 5243520 | tf_op jit(solution)/shard_map/jit(_take)/select_n | solution.py:136
  33.3 5.9 %all-to-all-start.1 = ((f32[4,128,5,256]{3,0,2,1:T(4,128)}), f32[4,128,5,256]{3,0,2,1:T(4,128)}, u32[]{:S(2)}, u32[]{:S(2)}) async-start(f32[4,128,5,256]{3,0,2,1:T(4,128)} %broadcast_select_fusion), calls=%async_computation.1 | async-start | bytes 5242880 | tf_op jit(solution)/shard_map/all_to_all | solution.py:97
  41.2 2.8 gather_fusion.1
  44.0 2.4 select_bitcast_fusion
  47.6 27.2 %all-to-all-done.1 = f32[4,128,5,256]{3,0,2,1:T(4,128)} async-done(((f32[4,128,5,256]{3,0,2,1:T(4,128)}), f32[4,128,5,256]{3,0,2,1:T(4,128)}, u32[]{:S(2)}, u32[]{:S(2)}) %all-to-all-start.1) | async-done | bytes 2621472 | tf_op jit(solution)/shard_map/all_to_all | solution.py:97
  76.7 286.6 %while.16 = (s32[]{:T(128)}, f32[3,640,128]{2,1,0:T(8,128)S(1)}, f32[3,640,256]{2,0,1:T(4,128)}, f32[640,128]{1,0:T(8,128)S(1)}, f32[3,640,128]{2,1,0:T(8,128)},...) while((s32[]{:T(128)}, f32[3,640,128]{2,1,0:T(8,128)S(1)}, ...), condition=%wide.region_5.6_spmd.clone, body=%wide.region_0.5_spmd.sunk.clone.sunk | while | flops 32518464 | bytes 20851232 | solution.py:84
  81.0 2.3 fusion.42
  84.2 4.6 %fusion.43 = (f32[3,32,256]{2,1,0:T(8,128)S(1)}, f32[3,32,128]{2,1,0:T(8,128)S(1)}) fusion(f32[32,128,256]{2,1,0:T(8,128)S(1)} %multiply_multiply_fusion.2, f32[3,32,256]{2,1,0:T(8,128)S(1)} %copy.81, f32[3,32,128]{2,1,0:T(8,128)S(1)} %constant_dynamic-slice_fusion.10), kind=kLoop, calls=%fused_computation.5.clone.1 | loop fusion | flops 12546048 | bytes 4489216 | tf_op jit(solution)/shard_map/while/body/eval_jaxpr/reduce_sum | solution.py:58
  95.3 2.3 fusion.42
  98.6 4.6 %fusion.43 = (f32[3,32,256]{2,1,0:T(8,128)S(1)}, f32[3,32,128]{2,1,0:T(8,128)S(1)}) fusion(f32[32,128,256]{2,1,0:T(8,128)S(1)} %multiply_multiply_fusion.2, f32[3,32,256]{2,1,0:T(8,128)S(1)} %copy.81, f32[3,32,128]{2,1,0:T(8,128)S(1)} %constant_dynamic-slice_fusion.10), kind=kLoop, calls=%fused_computation.5.clone.1 | loop fusion | flops 12546048 | bytes 4489216 | tf_op jit(solution)/shard_map/while/body/eval_jaxpr/reduce_sum | solution.py:58
  109.7 2.3 fusion.42
  112.9 4.6 %fusion.43 = (f32[3,32,256]{2,1,0:T(8,128)S(1)}, f32[3,32,128]{2,1,0:T(8,128)S(1)}) fusion(f32[32,128,256]{2,1,0:T(8,128)S(1)} %multiply_multiply_fusion.2, f32[3,32,256]{2,1,0:T(8,128)S(1)} %copy.81, f32[3,32,128]{2,1,0:T(8,128)S(1)} %constant_dynamic-slice_fusion.10), kind=kLoop, calls=%fused_computation.5.clone.1 | loop fusion | flops 12546048 | bytes 4489216 | tf_op jit(solution)/shard_map/while/body/eval_jaxpr/reduce_sum | solution.py:58
  124.0 2.3 fusion.42
  127.2 4.6 %fusion.43 = (f32[3,32,256]{2,1,0:T(8,128)S(1)}, f32[3,32,128]{2,1,0:T(8,128)S(1)}) fusion(f32[32,128,256]{2,1,0:T(8,128)S(1)} %multiply_multiply_fusion.2, f32[3,32,256]{2,1,0:T(8,128)S(1)} %copy.81, f32[3,32,128]{2,1,0:T(8,128)S(1)} %constant_dynamic-slice_fusion.10), kind=kLoop, calls=%fused_computation.5.clone.1 | loop fusion | flops 12546048 | bytes 4489216 | tf_op jit(solution)/shard_map/while/body/eval_jaxpr/reduce_sum | solution.py:58
  138.3 2.3 fusion.42
  141.6 4.6 %fusion.43 = (f32[3,32,256]{2,1,0:T(8,128)S(1)}, f32[3,32,128]{2,1,0:T(8,128)S(1)}) fusion(f32[32,128,256]{2,1,0:T(8,128)S(1)} %multiply_multiply_fusion.2, f32[3,32,256]{2,1,0:T(8,128)S(1)} %copy.81, f32[3,32,128]{2,1,0:T(8,128)S(1)} %constant_dynamic-slice_fusion.10), kind=kLoop, calls=%fused_computation.5.clone.1 | loop fusion | flops 12546048 | bytes 4489216 | tf_op jit(solution)/shard_map/while/body/eval_jaxpr/reduce_sum | solution.py:58
  152.6 2.3 fusion.42
  155.9 4.6 %fusion.43 = (f32[3,32,256]{2,1,0:T(8,128)S(1)}, f32[3,32,128]{2,1,0:T(8,128)S(1)}) fusion(f32[32,128,256]{2,1,0:T(8,128)S(1)} %multiply_multiply_fusion.2, f32[3,32,256]{2,1,0:T(8,128)S(1)} %copy.81, f32[3,32,128]{2,1,0:T(8,128)S(1)} %constant_dynamic-slice_fusion.10), kind=kLoop, calls=%fused_computation.5.clone.1 | loop fusion | flops 12546048 | bytes 4489216 | tf_op jit(solution)/shard_map/while/body/eval_jaxpr/reduce_sum | solution.py:58
  167.0 2.3 fusion.42
  170.2 4.6 %fusion.43 = (f32[3,32,256]{2,1,0:T(8,128)S(1)}, f32[3,32,128]{2,1,0:T(8,128)S(1)}) fusion(f32[32,128,256]{2,1,0:T(8,128)S(1)} %multiply_multiply_fusion.2, f32[3,32,256]{2,1,0:T(8,128)S(1)} %copy.81, f32[3,32,128]{2,1,0:T(8,128)S(1)} %constant_dynamic-slice_fusion.10), kind=kLoop, calls=%fused_computation.5.clone.1 | loop fusion | flops 12546048 | bytes 4489216 | tf_op jit(solution)/shard_map/while/body/eval_jaxpr/reduce_sum | solution.py:58
  181.3 2.3 fusion.42
  184.6 4.6 %fusion.43 = (f32[3,32,256]{2,1,0:T(8,128)S(1)}, f32[3,32,128]{2,1,0:T(8,128)S(1)}) fusion(f32[32,128,256]{2,1,0:T(8,128)S(1)} %multiply_multiply_fusion.2, f32[3,32,256]{2,1,0:T(8,128)S(1)} %copy.81, f32[3,32,128]{2,1,0:T(8,128)S(1)} %constant_dynamic-slice_fusion.10), kind=kLoop, calls=%fused_computation.5.clone.1 | loop fusion | flops 12546048 | bytes 4489216 | tf_op jit(solution)/shard_map/while/body/eval_jaxpr/reduce_sum | solution.py:58
  195.6 2.3 fusion.42
  198.9 4.6 %fusion.43 = (f32[3,32,256]{2,1,0:T(8,128)S(1)}, f32[3,32,128]{2,1,0:T(8,128)S(1)}) fusion(f32[32,128,256]{2,1,0:T(8,128)S(1)} %multiply_multiply_fusion.2, f32[3,32,256]{2,1,0:T(8,128)S(1)} %copy.81, f32[3,32,128]{2,1,0:T(8,128)S(1)} %constant_dynamic-slice_fusion.10), kind=kLoop, calls=%fused_computation.5.clone.1 | loop fusion | flops 12546048 | bytes 4489216 | tf_op jit(solution)/shard_map/while/body/eval_jaxpr/reduce_sum | solution.py:58
  210.0 2.3 fusion.42
  213.2 4.6 %fusion.43 = (f32[3,32,256]{2,1,0:T(8,128)S(1)}, f32[3,32,128]{2,1,0:T(8,128)S(1)}) fusion(f32[32,128,256]{2,1,0:T(8,128)S(1)} %multiply_multiply_fusion.2, f32[3,32,256]{2,1,0:T(8,128)S(1)} %copy.81, f32[3,32,128]{2,1,0:T(8,128)S(1)} %constant_dynamic-slice_fusion.10), kind=kLoop, calls=%fused_computation.5.clone.1 | loop fusion | flops 12546048 | bytes 4489216 | tf_op jit(solution)/shard_map/while/body/eval_jaxpr/reduce_sum | solution.py:58
  224.3 2.3 fusion.42
  227.5 4.6 %fusion.43 = (f32[3,32,256]{2,1,0:T(8,128)S(1)}, f32[3,32,128]{2,1,0:T(8,128)S(1)}) fusion(f32[32,128,256]{2,1,0:T(8,128)S(1)} %multiply_multiply_fusion.2, f32[3,32,256]{2,1,0:T(8,128)S(1)} %copy.81, f32[3,32,128]{2,1,0:T(8,128)S(1)} %constant_dynamic-slice_fusion.10), kind=kLoop, calls=%fused_computation.5.clone.1 | loop fusion | flops 12546048 | bytes 4489216 | tf_op jit(solution)/shard_map/while/body/eval_jaxpr/reduce_sum | solution.py:58
  238.6 2.3 fusion.42
  241.8 4.6 %fusion.43 = (f32[3,32,256]{2,1,0:T(8,128)S(1)}, f32[3,32,128]{2,1,0:T(8,128)S(1)}) fusion(f32[32,128,256]{2,1,0:T(8,128)S(1)} %multiply_multiply_fusion.2, f32[3,32,256]{2,1,0:T(8,128)S(1)} %copy.81, f32[3,32,128]{2,1,0:T(8,128)S(1)} %constant_dynamic-slice_fusion.10), kind=kLoop, calls=%fused_computation.5.clone.1 | loop fusion | flops 12546048 | bytes 4489216 | tf_op jit(solution)/shard_map/while/body/eval_jaxpr/reduce_sum | solution.py:58
  256.2 4.6 %fusion.43 = (f32[3,32,256]{2,1,0:T(8,128)S(1)}, f32[3,32,128]{2,1,0:T(8,128)S(1)}) fusion(f32[32,128,256]{2,1,0:T(8,128)S(1)} %multiply_multiply_fusion.2, f32[3,32,256]{2,1,0:T(8,128)S(1)} %copy.81, f32[3,32,128]{2,1,0:T(8,128)S(1)} %constant_dynamic-slice_fusion.10), kind=kLoop, calls=%fused_computation.5.clone.1 | loop fusion | flops 12546048 | bytes 4489216 | tf_op jit(solution)/shard_map/while/body/eval_jaxpr/reduce_sum | solution.py:58
  270.5 4.6 %fusion.43 = (f32[3,32,256]{2,1,0:T(8,128)S(1)}, f32[3,32,128]{2,1,0:T(8,128)S(1)}) fusion(f32[32,128,256]{2,1,0:T(8,128)S(1)} %multiply_multiply_fusion.2, f32[3,32,256]{2,1,0:T(8,128)S(1)} %copy.81, f32[3,32,128]{2,1,0:T(8,128)S(1)} %constant_dynamic-slice_fusion.10), kind=kLoop, calls=%fused_computation.5.clone.1 | loop fusion | flops 12546048 | bytes 4489216 | tf_op jit(solution)/shard_map/while/body/eval_jaxpr/reduce_sum | solution.py:58
  281.6 2.3 fusion.42
  284.8 4.6 %fusion.43 = (f32[3,32,256]{2,1,0:T(8,128)S(1)}, f32[3,32,128]{2,1,0:T(8,128)S(1)}) fusion(f32[32,128,256]{2,1,0:T(8,128)S(1)} %multiply_multiply_fusion.2, f32[3,32,256]{2,1,0:T(8,128)S(1)} %copy.81, f32[3,32,128]{2,1,0:T(8,128)S(1)} %constant_dynamic-slice_fusion.10), kind=kLoop, calls=%fused_computation.5.clone.1 | loop fusion | flops 12546048 | bytes 4489216 | tf_op jit(solution)/shard_map/while/body/eval_jaxpr/reduce_sum | solution.py:58
  299.2 4.6 %fusion.43 = (f32[3,32,256]{2,1,0:T(8,128)S(1)}, f32[3,32,128]{2,1,0:T(8,128)S(1)}) fusion(f32[32,128,256]{2,1,0:T(8,128)S(1)} %multiply_multiply_fusion.2, f32[3,32,256]{2,1,0:T(8,128)S(1)} %copy.81, f32[3,32,128]{2,1,0:T(8,128)S(1)} %constant_dynamic-slice_fusion.10), kind=kLoop, calls=%fused_computation.5.clone.1 | loop fusion | flops 12546048 | bytes 4489216 | tf_op jit(solution)/shard_map/while/body/eval_jaxpr/reduce_sum | solution.py:58
  313.5 4.6 %fusion.43 = (f32[3,32,256]{2,1,0:T(8,128)S(1)}, f32[3,32,128]{2,1,0:T(8,128)S(1)}) fusion(f32[32,128,256]{2,1,0:T(8,128)S(1)} %multiply_multiply_fusion.2, f32[3,32,256]{2,1,0:T(8,128)S(1)} %copy.81, f32[3,32,128]{2,1,0:T(8,128)S(1)} %constant_dynamic-slice_fusion.10), kind=kLoop, calls=%fused_computation.5.clone.1 | loop fusion | flops 12546048 | bytes 4489216 | tf_op jit(solution)/shard_map/while/body/eval_jaxpr/reduce_sum | solution.py:58
  324.6 2.3 fusion.42
  327.8 4.6 %fusion.43 = (f32[3,32,256]{2,1,0:T(8,128)S(1)}, f32[3,32,128]{2,1,0:T(8,128)S(1)}) fusion(f32[32,128,256]{2,1,0:T(8,128)S(1)} %multiply_multiply_fusion.2, f32[3,32,256]{2,1,0:T(8,128)S(1)} %copy.81, f32[3,32,128]{2,1,0:T(8,128)S(1)} %constant_dynamic-slice_fusion.10), kind=kLoop, calls=%fused_computation.5.clone.1 | loop fusion | flops 12546048 | bytes 4489216 | tf_op jit(solution)/shard_map/while/body/eval_jaxpr/reduce_sum | solution.py:58
  338.9 2.3 fusion.42
  342.2 4.6 %fusion.43 = (f32[3,32,256]{2,1,0:T(8,128)S(1)}, f32[3,32,128]{2,1,0:T(8,128)S(1)}) fusion(f32[32,128,256]{2,1,0:T(8,128)S(1)} %multiply_multiply_fusion.2, f32[3,32,256]{2,1,0:T(8,128)S(1)} %copy.81, f32[3,32,128]{2,1,0:T(8,128)S(1)} %constant_dynamic-slice_fusion.10), kind=kLoop, calls=%fused_computation.5.clone.1 | loop fusion | flops 12546048 | bytes 4489216 | tf_op jit(solution)/shard_map/while/body/eval_jaxpr/reduce_sum | solution.py:58
  353.3 2.3 fusion.42
  356.5 4.6 %fusion.43 = (f32[3,32,256]{2,1,0:T(8,128)S(1)}, f32[3,32,128]{2,1,0:T(8,128)S(1)}) fusion(f32[32,128,256]{2,1,0:T(8,128)S(1)} %multiply_multiply_fusion.2, f32[3,32,256]{2,1,0:T(8,128)S(1)} %copy.81, f32[3,32,128]{2,1,0:T(8,128)S(1)} %constant_dynamic-slice_fusion.10), kind=kLoop, calls=%fused_computation.5.clone.1 | loop fusion | flops 12546048 | bytes 4489216 | tf_op jit(solution)/shard_map/while/body/eval_jaxpr/reduce_sum | solution.py:58
  363.4 5.9 %all-to-all-start.2 = ((f32[3,128,5,256]{3,0,2,1:T(4,128)}), f32[3,128,5,256]{3,0,2,1:T(4,128)}, u32[]{:S(2)}, u32[]{:S(2)}) async-start(f32[3,128,5,256]{3,0,2,1:T(4,128)} %bitcast.73), calls=%async_computation.2 | async-start | bytes 5242880 | tf_op jit(solution)/shard_map/all_to_all | solution.py:110
  373.1 31.6 %all-to-all-done.2 = f32[3,128,5,256]{3,0,2,1:T(4,128)} async-done(((f32[3,128,5,256]{3,0,2,1:T(4,128)}), f32[3,128,5,256]{3,0,2,1:T(4,128)}, u32[]{:S(2)}, u32[]{:S(2)}) %all-to-all-start.2) | async-done | bytes 1966112 | tf_op jit(solution)/shard_map/all_to_all | solution.py:110
  404.8 3.5 fusion.12
  (580 shorter events, 170.0 us)
Async XLA Ops:
  0.6 40.6 %copy-start = (f32[3,65536]{1,0:T(4,128)S(1)}, f32[3,65536]{1,0:T(4,128)}, u32[]{:S(2)}) copy-start(f32[3,65536]{1,0:T(4,128)} %param.10) | copy-start | bytes 2359300
  2.2 20.6 %all-to-all-start = ((s32[128,1,5]{2,1,0:T(1,128)}), s32[128,1,5]{2,1,0:T(1,128)S(1)}, u32[]{:S(2)}, u32[]{:S(2)}) async-start(s32[128,1,5]{2,1,0:T(1,128)} %bitcast.3), calls=%async_computation | async-start | bytes 131072 | tf_op jit(solution)/shard_map/all_to_all | solution.py:127
  33.3 5.9 %copy-start.6 = (s32[128]{0:T(128)S(1)}, s32[128]{0:T(128)}, u32[]{:S(2)}) copy-start(s32[128]{0:T(128)} %param.16) | copy-start | bytes 1540
  33.3 6.2 %copy-start.2 = (s32[640]{0:T(1024)S(1)}, s32[640]{0:T(1024)}, u32[]{:S(2)}) copy-start(s32[640]{0:T(1024)} %param.14) | copy-start | bytes 7684
  33.3 6.2 %copy-start.1 = (f32[65536]{0:T(1024)S(1)}, f32[65536]{0:T(1024)}, u32[]{:S(2)}) copy-start(f32[65536]{0:T(1024)} %param.11) | copy-start | bytes 786436
  33.3 41.5 %all-to-all-start.1 = ((f32[4,128,5,256]{3,0,2,1:T(4,128)}), f32[4,128,5,256]{3,0,2,1:T(4,128)}, u32[]{:S(2)}, u32[]{:S(2)}) async-start(f32[4,128,5,256]{3,0,2,1:T(4,128)} %broadcast_select_fusion), calls=%async_computation.1 | async-start | bytes 5242880 | tf_op jit(solution)/shard_map/all_to_all | solution.py:97
  47.4 29.4 %copy-start.4 = (f32[4]{0:T(128)S(1)}, f32[4]{0:T(128)}, u32[]{:S(2)}) copy-start(f32[4]{0:T(128)} %constant.130.clone..sunk.2) | copy-start | bytes 52
  89.5 1.5 copy-start.5
  103.8 1.6 copy-start.5
  118.2 1.6 copy-start.5
  132.5 1.6 copy-start.5
  146.8 1.6 copy-start.5
  161.2 1.6 copy-start.5
  175.5 1.6 copy-start.5
  189.8 1.6 copy-start.5
  204.2 1.5 copy-start.5
  218.5 1.6 copy-start.5
  232.8 1.5 copy-start.5
  247.1 1.6 copy-start.5
  261.5 1.6 copy-start.5
  275.8 1.5 copy-start.5
  290.1 1.6 copy-start.5
  304.5 1.6 copy-start.5
  318.8 1.6 copy-start.5
  333.1 1.6 copy-start.5
  347.5 1.6 copy-start.5
  361.8 1.6 copy-start.5
  363.4 6.1 %copy-start.3 = (s32[640]{0:T(1024)S(1)}, s32[640]{0:T(1024)}, u32[]{:S(2)}) copy-start(s32[640]{0:T(1024)} %param.14) | copy-start | bytes 7684
  363.4 41.4 %all-to-all-start.2 = ((f32[3,128,5,256]{3,0,2,1:T(4,128)}), f32[3,128,5,256]{3,0,2,1:T(4,128)}, u32[]{:S(2)}, u32[]{:S(2)}) async-start(f32[3,128,5,256]{3,0,2,1:T(4,128)} %bitcast.73), calls=%async_computation.2 | async-start | bytes 5242880 | tf_op jit(solution)/shard_map/all_to_all | solution.py:110
where the time goes:
time: 412 us; the launch traced here: 410 us
  other arithmetic  192 us (47%)
  local copies, waits for them, and re-layouts  105 us (25%)
  waiting for transfers between devices  66.5 us (16%)
  starting transfers between devices  23 us (6%)
  matrix products  19.6 us (5%)
    reduce_sum x20, other arithmetic, tile_forces(): sample_term = -jnp.sum(weighted, axis=2)  92.8 us
    reduce_sum x20, other arithmetic, tile_forces(): distance = jnp.sum(differ * differ, axis=0)  45.7 us
    all_to_all x1, waiting for transfers between devices, relay_back(): lax.all_to_all(payload.reshape(components, outer_count * inner_count, per...  31.6 us
    all_to_all x1, waiting for transfers between devices, relay_out(): lax.all_to_all(payload.reshape(components, outer_count * inner_count, per...  27.2 us
    slice x20, local copies, waits for them, and re-layouts, sample_blocks(): weights = patch_grid[3]  18.8 us
    mul x20, other arithmetic, tile_forces(): weights[:, :, None] * jnp.exp(-distance * inverse_width) * force_gain  18.5 us
    slice x20, local copies, waits for them, and re-layouts, sample_blocks(): patch_grid[:3] * weights[None]  18.3 us
    dynamic_update_slice x40, local copies, waits for them, and re-layouts, one_group(): lax.dynamic_update_slice_in_dim(master_slots, master_term, first_slot, 1)  17.2 us
  transfers between devices with their start and end apart: 3, of which 3 were waited for; matrix products, arithmetic and copies ran while one was open for 3% of the time, Pallas kernels for 0%

commit v1 on v0

v1 whole, which is shorter than its diff:
```python
import math

import jax
import jax.numpy as jnp
from jax import lax
from jax.experimental import pallas as pl
from jax.experimental.pallas import tpu as pltpu
from jax.sharding import Mesh
from jax.sharding import PartitionSpec as P

QP = 128
CAP = 5
SB = 512
MB = 256
MP = 256
PEERS = 64
PER = 2 * CAP
GROUP = 4
FROWS = 32

f32 = jnp.float32
bf16 = jnp.bfloat16
SCALE = math.sqrt(2.0 * math.log2(math.e) / 3.0)
GAIN = 0.01 / SCALE

VMEM_SPEC = pl.BlockSpec(memory_space=pltpu.VMEM)
SMEM_SPEC = pl.BlockSpec(memory_space=pltpu.SMEM)


def bezier_table():
    params = (jnp.arange(4, dtype=f32) + 0.5) / 4.0
    powers = jnp.arange(4, dtype=f32)
    binomial = jnp.array([1.0, 3.0, 3.0, 1.0], dtype=f32)
    bernstein = (
        binomial[None, :]
        * params[:, None] ** powers[None, :]
        * (1.0 - params[:, None]) ** (3.0 - powers[None, :])
    )
    return (bernstein[:, None, :, None] * bernstein[None, :, None, :]).reshape(16, 16)


def dot(a, b, left, right):
    return lax.dot_general(a, b, (((left,), (right,)), ((), ())), preferred_element_type=f32)


def narrow(x):
    return x.astype(bf16).astype(f32)


def pack_kernel(ps, pm, cnt, coords, weight, out):
    lane = lax.broadcasted_iota(jnp.int32, (1, 128), 1)

    def one_peer(peer, unused):
        row = jnp.full((1, 128), -1, jnp.int32)
        for c in range(PER):
            slot = peer * PER + c
            block = ps[slot]
            out[peer, c, 0:3, :] = coords[block]
            out[peer, c, 3:4, :] = weight[pl.ds(block, 1), :]
            live = (c % CAP) < cnt[2 * peer + c // CAP]
            row = jnp.where(lane == c, jnp.where(live, pm[slot], -1), row)
        out[peer, PER, 0:1, :] = row.astype(f32)
        return unused

    lax.fori_loop(0, PEERS, one_peer, 0)


def pack(ps, pm, cnt, coords, weight):
    return pl.pallas_call(
        pack_kernel,
        name="pack",
        out_shape=jax.ShapeDtypeStruct((PEERS, PER + 1, 4, QP), f32),
        in_specs=[SMEM_SPEC] * 3 + [VMEM_SPEC] * 2,
        out_specs=VMEM_SPEC,
    )(ps, pm, cnt, coords, weight)


def front(tile, y8, keep):
    wide = jnp.concatenate([tile, tile], axis=0)
    rows = lax.broadcasted_iota(jnp.int32, (8, 128), 0)
    centre = pltpu.roll(y8[:, :128], 3, 0)
    xs = jnp.where(rows < 3, (wide - centre) * SCALE, 0.0)
    norm = -0.5 * jnp.sum(xs * xs, axis=0, keepdims=True)
    weight = wide[3:4]
    x8 = jnp.where(rows == 3, norm, jnp.where(rows == 4, 1.0, xs))
    x1 = narrow(x8)
    x2 = narrow(x8 - x1)
    x3 = x8 - x1 - x2
    y1 = narrow(y8)
    y2 = narrow(y8 - y1)
    y3 = y8 - y1 - y2
    left = jnp.concatenate([x1, x1, x2, x2, x1, x3], axis=0).astype(bf16)
    lead = jnp.concatenate([y1, y2], axis=0).astype(bf16)
    tail = jnp.concatenate([y3, y1], axis=0).astype(bf16)
    right = jnp.concatenate([lead, lead, tail], axis=0)
    gauss = jnp.exp2(dot(left, right, 0, 0))
    high = gauss.astype(bf16)
    low = (gauss - high.astype(f32)).astype(bf16)
    ax = x8 * (weight * keep)
    ax1 = narrow(ax)
    ax = jnp.concatenate([ax1, ax - ax1], axis=0).astype(bf16)
    return high, low, ax, lead, xs, jnp.broadcast_to(weight * GAIN, (8, 128))


PIECES = 6


def force_kernel(meta, core, tiles, y8, force, acc, entries, *buffers):
    acc[...] = jnp.zeros_like(acc)
    mine = core[0]
    entries[0] = 0

    def list_peer(peer, count):
        for c in range(PER):
            block = meta[peer * PER + c]
            half = (c // CAP) ^ mine
            entries[count] = (peer * 16 + c) | ((half * MB + block) << 10)
            count = count + (block >= 0).astype(jnp.int32)
        return count

    total = lax.fori_loop(0, PEERS, list_peer, jnp.int32(0))
    last = entries[jnp.maximum(total - 1, 0)]
    for k in range(3 * GROUP):
        entries[total + k] = last | (1 << 20)
    trips = (total + 2 * GROUP - 1) // (2 * GROUP)

    def unpack(index):
        entry = entries[index]
        return (entry >> 4) & 63, entry & 15, (entry >> 10) & 511, entry >> 20

    def stage_front(group, which):
        for u in range(GROUP):
            peer, c, block, extra = unpack(group * GROUP + u)
            keep = (1 - extra).astype(f32)
            base = (which * GROUP + u) * PIECES
            values = front(tiles[peer, c], y8[block], keep)
            for k in range(PIECES):
                buffers[base + k][...] = values[k]

    def stage_back(group, which):
        for u in range(GROUP):
            peer, c, block, extra = unpack(group * GROUP + u)
            base = (which * GROUP + u) * PIECES
            high, low, ax, lead, xs, scale = [buffers[base + k][...] for k in range(PIECES)]
            q = dot(ax, high, 1, 0) + dot(ax, low, 1, 0)
            f = dot(lead, high, 1, 1) + dot(lead, low, 1, 1)
            f = f[0:8] + f[8:16]
            f = scale * (xs * f[3:4] - f)
            force[peer, pl.ds(c * 3, 3), :] = f[0:3]
            acc[block] = acc[block] + (q[0:8] + q[8:16])

    stage_front(0, 0)

    def trip(i, unused):
        stage_front(2 * i + 1, 1)
        stage_back(2 * i, 0)
        stage_front(2 * i + 2, 0)
        stage_back(2 * i + 1, 1)
        return unused

    lax.fori_loop(0, trips, trip, 0)


def forces(meta, core, tiles, y8):
    one = [
        pltpu.VMEM((QP, MP), bf16),
        pltpu.VMEM((QP, MP), bf16),
        pltpu.VMEM((16, QP), bf16),
        pltpu.VMEM((16, MP), bf16),
        pltpu.VMEM((8, QP), f32),
        pltpu.VMEM((8, QP), f32),
    ]
    return pl.pallas_call(
        force_kernel,
        name="forces",
        out_shape=(
            jax.ShapeDtypeStruct((PEERS, FROWS, QP), f32),
            jax.ShapeDtypeStruct((2 * MB, 8, MP), f32),
        ),
        in_specs=[SMEM_SPEC, SMEM_SPEC, VMEM_SPEC, VMEM_SPEC],
        out_specs=(VMEM_SPEC, VMEM_SPEC),
        scratch_shapes=[pltpu.SMEM((PEERS * PER + 3 * GROUP,), jnp.int32)] + one * (2 * GROUP),
    )(meta, core, tiles, y8)


def gather_kernel(ps, cnt, force, out, even, odd):
    even[...] = jnp.zeros_like(even)
    odd[...] = jnp.zeros_like(odd)

    def one_peer(peer, unused):
        for c in range(PER):
            live = (c % CAP) < cnt[2 * peer + c // CAP]
            block = jnp.where(live, ps[peer * PER + c], SB)
            total = odd if c % 2 else even
            total[block] = total[block] + force[peer, 3 * c : 3 * c + 3, :]
        return unused

    lax.fori_loop(0, PEERS, one_peer, 0)
    out[...] = even[0:SB] + odd[0:SB]


def gather_forces(ps, cnt, force):
    return pl.pallas_call(
        gather_kernel,
        name="gather",
        out_shape=jax.ShapeDtypeStruct((SB, 3, QP), f32),
        in_specs=[SMEM_SPEC] * 2 + [VMEM_SPEC],
        out_specs=VMEM_SPEC,
        scratch_shapes=[pltpu.VMEM((SB + 1, 3, QP), f32)] * 2,
    )(ps, cnt, force)


def exchange(x):
    return lax.all_to_all(x, ("gx", "g"), split_axis=0, concat_axis=0, tiled=True)


def swap(x):
    return lax.ppermute(x, "core", [(0, 1), (1, 0)])


def spread_table():
    return jnp.kron(jnp.eye(16, dtype=f32), bezier_table())


def body(slave_coords, slave_weight, master_ctrl, master_wt, pair_slave, pair_master, pair_count):
    coords = slave_coords.reshape(3, SB, QP).transpose(1, 0, 2)
    payload = pack(
        pair_slave, pair_master, pair_count, coords, slave_weight.reshape(SB, QP)
    )
    tiles = exchange(payload)

    own = jnp.concatenate([master_ctrl, master_wt[None, :]], axis=0).reshape(4, MB, MP)
    both = jnp.concatenate([own, swap(own)], axis=1)
    table = spread_table()
    lifted = jnp.concatenate([both[:3] * both[3:], both[3:]], axis=0)
    summed = jnp.einsum("cbk,jk->cbj", lifted, table, precision=lax.Precision.HIGHEST)
    samples = summed[:3] / summed[3:]
    centre = jnp.mean(samples, axis=2, keepdims=True)
    scaled = (samples - centre) * SCALE
    norm = -0.5 * jnp.sum(scaled * scaled, axis=0, keepdims=True)
    y8 = jnp.concatenate(
        [scaled, jnp.ones_like(norm), norm, jnp.broadcast_to(centre, scaled.shape)], axis=0
    ).transpose(1, 0, 2)

    core = lax.axis_index("core").reshape(1).astype(jnp.int32)
    meta = tiles[:, PER, 0, :PER].astype(jnp.int32).reshape(PEERS * PER)
    force, acc = forces(meta, core, tiles, y8)

    force = exchange(force)
    slave_force = gather_forces(pair_slave, pair_count, force)

    acc = acc.transpose(1, 0, 2)
    q = (scaled * acc[4:5] - acc[0:3]) * GAIN
    q = q[:, :MB] + swap(q[:, MB:])
    master_force = (
        jnp.einsum(
            "cbj,jk->cbk", q / summed[3:, :MB], table, precision=lax.Precision.HIGHEST
        )
        * own[3:]
    )
    return (
        slave_force.transpose(1, 0, 2).reshape(3, SB * QP),
        master_force.reshape(3, MB * MP),
    )


def solution(mesh):
    split = Mesh(mesh.devices.reshape(4, 16, 2), ("gx", "g", "core"))
    every = ("gx", "g", "core")
    wide, flat = P(None, every), P(every)
    return jax.shard_map(
        body,
        mesh=split,
        in_specs=(wide, flat, wide, flat, flat, flat, flat),
        out_specs=(wide, wide),
        check_vma=False,
    )
```

time: 412 us -> 131 us (0.32)
  other arithmetic: 192 us -> 18.2 us
  local copies, waits for them, and re-layouts: 105 us -> 20.3 us
  waiting for transfers between devices: 66.5 us -> 14.6 us
  starting transfers between devices: 23 us -> 51.4 us
  Pallas kernels: 0 us -> 22.7 us
  matrix products: 19.6 us -> 2.85 us
    reduce_sum x60 -> x2, other arithmetic: 152 us -> 3.56 us  [the longest x1 2.88 us: body(): norm = -0.5 * jnp.sum(scaled * scaled, axis=0, keepdims=True)]
    all_to_all x3 -> x2, waiting for transfers between devices: 66.5 us -> 14.6 us  [exchange(): lax.all_to_all(x, ('gx', 'g'), split_axis=0, concat_axis=0, tiled=True)]
    slice x40 -> x3, local copies, waits for them, and re-layouts: 37.1 us -> 2.48 us  [the longest x1 1.27 us: body(): samples = summed[:3] / summed[3:]]
    all_to_all x3 -> x2, starting transfers between devices: 23 us -> 51.3 us  [exchange(): lax.all_to_all(x, ('gx', 'g'), split_axis=0, concat_axis=0, tiled=True)]
    pallas_call x0 -> x3, Pallas kernels: none -> 22.7 us  [the longest x1 13.8 us: forces(): pl.pallas_call(force_kernel, name='forces', out_shape=(jax.ShapeDtypeStru...]
    dynamic_update_slice x60 -> x0, local copies, waits for them, and re-layouts: 17.3 us -> none  [the longest x40 17.2 us: one_group(): lax.dynamic_update_slice_in_dim(master_slots, master_term, first_slot, 1)]
    dot_general x42 -> x2, matrix products: 19.6 us -> 2.85 us  [the longest x1 2.04 us: body(): jnp.einsum('cbk,jk->cbj', lifted, table, precision=lax.Precision.HIGHEST)]
    dynamic_slice x40 -> x0, local copies, waits for them, and re-layouts: 16.5 us -> none  [the longest x20 16.2 us: one_group(): lax.dynamic_slice_in_dim(points, first_slot, group_size, 1)]
  transfers between devices with their start and end apart: 3 -> 4, of which waited for: 3 -> 2; matrix products, arithmetic and copies ran while one was open for 3% -> 20% of each run, Pallas kernels for 0% -> 3%
where the time goes in v1:
time: 131 us
  starting transfers between devices  51.4 us (39%)
  Pallas kernels  22.7 us (17%)
  local copies, waits for them, and re-layouts  20.3 us (15%)
  other arithmetic  18.2 us (14%)
  waiting for transfers between devices  14.6 us (11%)
  matrix products  2.85 us (2%)
    all_to_all x2, starting transfers between devices, exchange(): lax.all_to_all(x, ('gx', 'g'), split_axis=0, concat_axis=0, tiled=True)  51.3 us
    all_to_all x2, waiting for transfers between devices, exchange(): lax.all_to_all(x, ('gx', 'g'), split_axis=0, concat_axis=0, tiled=True)  14.6 us
    pallas_call x1, Pallas kernels, forces(): pl.pallas_call(force_kernel, name='forces', out_shape=(jax.ShapeDtypeStru...  13.8 us
    unnamed x16, local copies, waits for them, and re-layouts  8.53 us
    mul x2, other arithmetic, body(): q = (scaled * acc[4:5] - acc[0:3]) * GAIN  5.68 us
    pallas_call x1, Pallas kernels, gather_forces(): pl.pallas_call(gather_kernel, name='gather', out_shape=jax.ShapeDtypeStru...  4.62 us
    pallas_call x1, Pallas kernels, pack(): pl.pallas_call(pack_kernel, name='pack', out_shape=jax.ShapeDtypeStruct((...  4.29 us
    div x2, local copies, waits for them, and re-layouts, body(): q / summed[3:, :MB]  3.44 us
  transfers between devices with their start and end apart: 4, of which 2 were waited for; matrix products, arithmetic and copies ran while one was open for 20% of the time, Pallas kernels for 3%

profile of v1, /device:TPU:0, one launch (start us, length us, event | category | flops | bytes accessed | tf_op | source)
XLA Modules:
  0.0 130.9 jit_solution(14485191244807016168)
XLA Ops:
  0.6 1.0 concatenate.18
  1.7 1.4 %bitcast_dynamic-update-slice_fusion = f32[4,256,256]{2,1,0:T(8,128)S(1)} fusion(f32[1,3,256,256]{3,1,2,0:T(4,128)} %bitcast.34), kind=kLoop, calls=%fused_computation.19 | loop fusion | bytes 1572864
  3.1 0.1 collective-permute-start
  3.2 4.3 %pack.1 = f32[64,11,4,128]{3,2,1,0:T(4,128)} custom-call(s32[640]{0:T(1024)} %ps.3, s32[640]{0:T(1024)} %pm.1, s32[128]{0:T(128)} %cnt.3, f32[512,3,128]{2,1,0:T(4,128)} %bitcast.37, f32[512,128]{1,0:T(8,128)} %bitcast.38), custom_call_target="tpu_custom_call" | custom-call | tf_op jit(solution)/shard_map/pack/pallas_call | solution.py:69
  7.5 11.9 %all-to-all-start = ((f32[64,11,4,128]{3,2,1,0:T(4,128)}), f32[64,11,4,128]{3,2,1,0:T(4,128)}, u32[]{:S(2)}, u32[]{:S(2)}) async-start(f32[64,11,4,128]{3,2,1,0:T(4,128)} %pack.1), calls=%async_computation | async-start | bytes 2883584 | tf_op jit(solution)/shard_map/all_to_all | solution.py:214
  19.4 0.0 copy-done.5
  19.4 0.1 power_multiply_fusion
  19.5 0.1 broadcast_multiply_fusion.3
  19.6 0.1 mul.147
  19.7 0.2 broadcast_multiply_fusion
  19.9 0.9 reshape.210
  20.8 0.1 pad.1.clone
  20.9 0.0 collective-permute-done
  20.9 1.0 pad_maximum_fusion
  21.9 1.3 fusion.6
  23.2 2.0 %fusion.1 = f32[4,512,256]{1,2,0:T(8,128)S(1)} fusion(f32[256,256,1]{1,0,2:T(8,128)S(1)} %reshape.210, f32[1,512,256]{2,1,0:T(8,128)S(1)} %pad_maximum_fusion, f32[3,512,256]{2,1,0:T(8,128)S(1)} %fusion.6), kind=kOutput, calls=%fused_computation.5 | convolution fusion | flops 1611137024 | bytes 4456448 | tf_op jit(solution)/shard_map/cbk,jk->cbj/dot_general | solution.py:236
  25.2 0.0 copy-start
  25.3 1.3 copy-done
  26.6 1.3 slice.46
  27.8 0.2 copy.25
  28.0 2.0 %copy.31 = f32[3,512,256]{2,0,1:T(4,128)S(1)} copy(f32[3,512,256]{1,2,0:T(8,128)} %slice.46) | data formatting | bytes 3145728
  30.0 0.7 fusion.13
  30.7 2.9 %multiply_reduce_fusion = (f32[512,256]{1,0:T(8,128)S(1)}, f32[3,512,256]{2,0,1:T(4,128)S(1)}) fusion(f32[3,512]{0,1:T(8,128)S(1)} %broadcast_multiply_fusion.2, f32[3,512,256]{2,0,1:T(4,128)S(1)} %copy.31, f32[512,256]{1,0:T(8,128)S(1)} %copy.25), kind=kLoop, calls=%fused_computation.9 | loop fusion | flops 1835008 | bytes 4200448 | tf_op jit(solution)/shard_map/reduce_sum | solution.py:240
  33.7 0.4 mul.156
  34.0 0.6 sub.29
  34.6 3.3 %maximum_bitcast_fusion.y8 = f32[512,8,256]{2,1,0:T(8,128)} fusion(f32[3,512,256]{2,0,1:T(4,128)S(1)} %sub.29, f32[1,512,256]{2,0,1:T(1,128)S(1)} %mul.156, f32[3,512,256]{2,0,1:T(4,128)S(1)} %get-tuple-element.7, f32[8]{0:T(128)S(1)} %pad.1.clone), kind=kLoop, calls=%fused_computation | loop fusion | flops 3145728 | bytes 7864352 | tf_op jit(solution)/shard_map/transpose | solution.py:243
  38.0 4.7 %all-to-all-done.tiles = f32[64,11,4,128]{3,2,1,0:T(4,128)} async-done(((f32[64,11,4,128]{3,2,1,0:T(4,128)}), f32[64,11,4,128]{3,2,1,0:T(4,128)}, u32[]{:S(2)}, u32[]{:S(2)}) %all-to-all-start) | async-done | bytes 1441824 | tf_op jit(solution)/shard_map/all_to_all | solution.py:214
  42.7 1.0 fusion.10
  43.7 0.7 convert_element_type.15.meta
  44.4 13.8 %forces.1 = (f32[64,32,128]{2,1,0:T(8,128)}, f32[512,8,256]{2,1,0:T(8,128)}) custom-call(s32[640]{0:T(1024)} %convert_element_type.15.meta, s32[1]{0:T(128)} %bitcast.3.core, f32[64,11,4,128]{3,2,1,0:T(4,128)} %all-to-all-done.tiles, f32[512,8,256]{2,1,0:T(8,128)} %maximum_bitcast_fusion.y8), custom_call_target="tpu_custom_call" | custom-call | tf_op jit(solution)/shard_map/forces/pallas_call | solution.py:173
  58.2 2.8 %slice_multiply_fusion = f32[1,512,256]{2,0,1:T(1,128)S(1)} fusion(f32[8,512,256]{2,0,1:T(8,128)} %bitcast.32), kind=kLoop, calls=%fused_computation.21 | loop fusion | flops 131072 | bytes 1048576 | tf_op jit(solution)/shard_map/mul | solution.py:253
  61.1 2.9 %fusion = f32[3,512,256]{2,0,1:T(4,128)S(1)} fusion(f32[8,512,256]{2,0,1:T(8,128)} %bitcast.33, f32[512,256]{1,0:T(8,128)S(1)} %bitcast.31, f32[3,512]{0,1:T(8,128)S(1)} %broadcast_multiply_fusion.2, f32[3,512,256]{2,0,1:T(4,128)S(1)} %copy.31, f32[512,256]{1,0:T(8,128)S(1)} %copy.25), kind=kLoop, calls=%fused_computation.2 | loop fusion | flops 1966080 | bytes 5773312 | tf_op jit(solution)/shard_map/mul | solution.py:253
  64.0 1.3 %copy-done.1 = f32[3,512,256]{2,0,1:T(4,128)} copy-done((f32[3,512,256]{2,0,1:T(4,128)}, f32[3,512,256]{2,0,1:T(4,128)S(1)}, u32[]{:S(2)}) %copy-start.1) | copy-done | bytes 1572888
  65.3 0.2 slice.51
  65.5 1.0 copy.26
  66.5 0.0 collective-permute-start.1
  66.5 39.4 %all-to-all-start.1 = ((f32[64,32,128]{2,1,0:T(8,128)}), f32[64,32,128]{2,1,0:T(8,128)S(1)}, u32[]{:S(2)}, u32[]{:S(2)}) async-start(f32[64,32,128]{2,1,0:T(8,128)} %get-tuple-element.4), calls=%async_computation.1 | async-start | bytes 2097152 | tf_op jit(solution)/shard_map/all_to_all | solution.py:214
  105.9 1.7 %mul.164 = f32[256,256]{1,0:T(8,128)} reshape(f32[65536]{0:T(1024)} %param.11) | data formatting | bytes 524288 | tf_op jit(solution)/shard_map/mul | solution.py:256
  107.7 1.7 %slice_bitcast_fusion.1 = f32[256,256]{0,1:T(8,128)} fusion(f32[4,512,256]{1,2,0:T(8,128)} %copy-done), kind=kLoop, calls=%fused_computation.25 | loop fusion | bytes 524288 | tf_op jit(solution)/shard_map/div | solution.py:257
  109.3 1.8 %copy.28 = f32[256,256]{1,0:T(8,128)} copy(f32[256,256]{0,1:T(8,128)} %slice_bitcast_fusion.1) | data formatting | bytes 524288 | tf_op jit(solution)/shard_map/div | solution.py:257
  111.1 0.0 collective-permute-done.1
  111.1 2.0 %fusion.8 = f32[3,256,256]{2,0,1:T(4,128)S(1)} fusion(f32[3,512,256]{2,0,1:T(4,128)S(1)} %copy-done.2, f32[3,256,256]{2,1,0:T(8,128)} %collective-permute-done.1, f32[256,256]{1,0:T(8,128)} %copy.28), kind=kLoop, calls=%fused_computation.16 | loop fusion | flops 393216 | bytes 2621440 | tf_op jit(solution)/shard_map/div | solution.py:257
  113.1 0.0 copy-done.4
  113.1 0.8 fusion.7
  113.9 1.5 %copy.33 = f32[1,3,256,256]{3,1,2,0:T(4,128)} copy(f32[1,3,256,256]{3,2,1,0:T(8,128)S(1)} %fusion.7) | data formatting | bytes 1572864
  115.4 9.9 %all-to-all-done.1.force = f32[64,32,128]{2,1,0:T(8,128)S(1)} async-done(((f32[64,32,128]{2,1,0:T(8,128)}), f32[64,32,128]{2,1,0:T(8,128)S(1)}, u32[]{:S(2)}, u32[]{:S(2)}) %all-to-all-start.1) | async-done | bytes 1048608 | tf_op jit(solution)/shard_map/all_to_all | solution.py:214
  125.3 1.0 copy-done.3
  126.3 4.6 %gather.1 = f32[512,3,128]{2,1,0:T(4,128)} custom-call(s32[640]{0:T(1024)} %ps.3, s32[128]{0:T(128)} %cnt.3, f32[64,32,128]{2,1,0:T(8,128)} %copy-done.3), custom_call_target="tpu_custom_call" | custom-call | tf_op jit(solution)/shard_map/gather/pallas_call | solution.py:203
  (14 shorter events, 0.2 us)
Async XLA Ops:
  3.1 17.8 %collective-permute-start = (f32[4,256,256]{2,1,0:T(8,128)S(1)}, f32[4,256,256]{2,1,0:T(8,128)}, u32[]{:S(2)}, u32[]{:S(2)}) collective-permute-start(f32[4,256,256]{2,1,0:T(8,128)S(1)} %constant_dynamic-update-slice_fusion), channel_id=1, source_target_pairs={{0,1},{1,0},{2,3},{3,2},{4,5},{5,4},{6,7},{7,6},{8,9},{9,8},{10,11... | collective-permute-start | bytes 3145736 | tf_op jit(solution)/shard_map/ppermute | solution.py:218
  7.5 11.9 %copy-start.5 = (f32[4]{0:T(128)S(1)}, f32[4]{0:T(128)}, u32[]{:S(2)}) copy-start(f32[4]{0:T(128)} %constant.27.clone) | copy-start | bytes 52
  7.5 35.2 %all-to-all-start = ((f32[64,11,4,128]{3,2,1,0:T(4,128)}), f32[64,11,4,128]{3,2,1,0:T(4,128)}, u32[]{:S(2)}, u32[]{:S(2)}) async-start(f32[64,11,4,128]{3,2,1,0:T(4,128)} %pack.1), calls=%async_computation | async-start | bytes 2883584 | tf_op jit(solution)/shard_map/all_to_all | solution.py:214
  25.2 1.4 %copy-start = (f32[4,512,256]{1,2,0:T(8,128)}, f32[4,512,256]{1,2,0:T(8,128)S(1)}, u32[]{:S(2)}) copy-start(f32[4,512,256]{1,2,0:T(8,128)S(1)} %fusion.1) | copy-start | bytes 6291460
  63.9 1.4 %copy-start.1 = (f32[3,512,256]{2,0,1:T(4,128)}, f32[3,512,256]{2,0,1:T(4,128)S(1)}, u32[]{:S(2)}) copy-start(f32[3,512,256]{2,0,1:T(4,128)S(1)} %fusion) | copy-start | bytes 4718596
  66.5 44.6 %copy-start.2 = (f32[3,512,256]{2,0,1:T(4,128)S(1)}, f32[3,512,256]{2,0,1:T(4,128)}, u32[]{:S(2)}) copy-start(f32[3,512,256]{2,0,1:T(4,128)} %copy-done.1) | copy-start | bytes 4718596
  66.5 44.6 %collective-permute-start.1 = (f32[3,256,256]{2,1,0:T(8,128)}, f32[3,256,256]{2,1,0:T(8,128)}, u32[]{:S(2)}, u32[]{:S(2)}) collective-permute-start(f32[3,256,256]{2,1,0:T(8,128)} %copy.26), channel_id=1, source_target_pairs={{0,1},{1,0},{2,3},{3,2},{4,5},{5,4},{6,7},{7,6},{8,9},{9,8},{10,11... | collective-permute-start | bytes 2359304 | tf_op jit(solution)/shard_map/ppermute | solution.py:218
  66.5 58.8 %all-to-all-start.1 = ((f32[64,32,128]{2,1,0:T(8,128)}), f32[64,32,128]{2,1,0:T(8,128)S(1)}, u32[]{:S(2)}, u32[]{:S(2)}) async-start(f32[64,32,128]{2,1,0:T(8,128)} %get-tuple-element.4), calls=%async_computation.1 | async-start | bytes 2097152 | tf_op jit(solution)/shard_map/all_to_all | solution.py:214
  111.1 2.0 %copy-start.4 = (f32[256,256]{1,0:T(8,128)S(1)}, f32[256,256]{1,0:T(8,128)}, u32[]{:S(2)}) copy-start(f32[256,256]{1,0:T(8,128)} %mul.164) | copy-start | bytes 786436
  125.3 1.0 copy-start.3

commit v2 on v1

v2 whole, which is shorter than its diff:
```python
import functools
import math

import jax
import jax.numpy as jnp
from jax import lax
from jax.experimental import pallas as pl
from jax.experimental.pallas import tpu as pltpu
from jax.sharding import Mesh
from jax.sharding import PartitionSpec as P

QP = 128
CAP = 5
SB = 512
MB = 256
MP = 256
PEERS = 64
GROUP = 4

f32 = jnp.float32
bf16 = jnp.bfloat16
fp8 = jnp.float8_e4m3fn
SCALE = math.sqrt(2.0 * math.log2(math.e) / 3.0)
GAIN = 0.01 / SCALE

VMEM_SPEC = pl.BlockSpec(memory_space=pltpu.VMEM)
ANY_SPEC = pl.BlockSpec(memory_space=pl.ANY)
SMEM_SPEC = pl.BlockSpec(memory_space=pltpu.SMEM)


def bezier_table():
    params = (jnp.arange(4, dtype=f32) + 0.5) / 4.0
    powers = jnp.arange(4, dtype=f32)
    binomial = jnp.array([1.0, 3.0, 3.0, 1.0], dtype=f32)
    bernstein = (
        binomial[None, :]
        * params[:, None] ** powers[None, :]
        * (1.0 - params[:, None]) ** (3.0 - powers[None, :])
    )
    return (bernstein[:, None, :, None] * bernstein[None, :, None, :]).reshape(16, 16)


def dot(a, b, left, right):
    return lax.dot_general(a, b, (((left,), (right,)), ((), ())), preferred_element_type=f32)


def narrow(x):
    return x.astype(bf16).astype(f32)


def pack_kernel(low, size, ps, pm, cnt, coords, weight, out):
    lane = lax.broadcasted_iota(jnp.int32, (1, 128), 1)

    def one_peer(peer, unused):
        row = jnp.zeros((1, 128), jnp.int32)
        for half in range(2):
            owner = 2 * peer + half
            for c in range(size):
                slot = owner * CAP + low + c
                block = ps[slot]
                spot = half * size + c
                out[peer, spot, 0:3, :] = coords[block]
                out[peer, spot, 3:4, :] = weight[pl.ds(block, 1), :]
                row = jnp.where(lane == spot, pm[slot], row)
            live = jnp.clip(cnt[owner] - low, 0, size)
            row = jnp.where(lane == 2 * size + half, live, row)
        out[peer, 2 * size, 0:1, :] = row.astype(f32)
        return unused

    lax.fori_loop(0, PEERS, one_peer, 0)


def pack(low, size, ps, pm, cnt, coords, weight):
    return pl.pallas_call(
        functools.partial(pack_kernel, low, size),
        name="pack",
        out_shape=jax.ShapeDtypeStruct((PEERS, 2 * size + 1, 4, QP), f32),
        in_specs=[SMEM_SPEC] * 3 + [VMEM_SPEC] * 2,
        out_specs=VMEM_SPEC,
    )(ps, pm, cnt, coords, weight)


def sample_kernel(own, other, y8):
    def eight(source, base):
        def one(i, unused):
            at = pl.ds(pl.multiple_of(i * 8, 8), 8)
            inverse = 1.0 / source[3, at, :]
            norm = jnp.zeros((8, MP), f32)
            spot = (base + i * 8) * 8
            for k in range(3):
                y = source[k, at, :] * inverse
                centre = jnp.sum(y, axis=1, keepdims=True) * (1.0 / MP)
                y = (y - centre) * SCALE
                norm = norm - 0.5 * (y * y)
                for h in range(2):
                    lanes = slice(128 * h, 128 * h + 128)
                    y8[h, pl.ds(spot + k, 8, stride=8), :] = y[:, lanes]
                    y8[h, pl.ds(spot + 5 + k, 8, stride=8), :] = jnp.broadcast_to(centre, (8, 128))
            for h in range(2):
                lanes = slice(128 * h, 128 * h + 128)
                y8[h, pl.ds(spot + 3, 8, stride=8), :] = jnp.ones((8, 128), f32)
                y8[h, pl.ds(spot + 4, 8, stride=8), :] = norm[:, lanes]
            return unused

        lax.fori_loop(0, MB // 8, one, 0, unroll=2)

    eight(own, 0)
    eight(other, MB)


def sample_tiles(own, other):
    return pl.pallas_call(
        sample_kernel,
        name="samples",
        out_shape=jax.ShapeDtypeStruct((2, 2 * MB * 8, 128), f32),
        in_specs=[VMEM_SPEC] * 2,
        out_specs=VMEM_SPEC,
    )(own, other)


def front(tile, y8, keep):
    wide = jnp.concatenate([tile, tile], axis=0)
    rows = lax.broadcasted_iota(jnp.int32, (8, 128), 0)
    centre = pltpu.roll(y8[:, :128], 3, 0)
    xs = jnp.where(rows < 3, (wide - centre) * SCALE, 0.0)
    norm = -0.5 * jnp.sum(xs * xs, axis=0, keepdims=True)
    weight = wide[3:4]
    x8 = jnp.where(rows == 3, norm, jnp.where(rows == 4, 1.0, xs))
    x1 = narrow(x8)
    x2 = narrow(x8 - x1)
    x3 = x8 - x1 - x2
    y1 = narrow(y8)
    y2 = narrow(y8 - y1)
    y3 = y8 - y1 - y2
    left = jnp.concatenate([x1, x1, x2, x2, x1, x3], axis=0).astype(bf16)
    lead = jnp.concatenate([y1, y2], axis=0).astype(bf16)
    tail = jnp.concatenate([y3, y1], axis=0).astype(bf16)
    right = jnp.concatenate([lead, lead, tail], axis=0)
    gauss = jnp.exp2(dot(left, right, 0, 0))
    high = gauss.astype(bf16)
    low = ((gauss - high.astype(f32)) * LIFT).astype(fp8)
    ax = x8 * (weight * keep)
    ax1 = narrow(ax)
    ax2 = jnp.concatenate([ax1, ax - ax1], axis=0).astype(bf16)
    ax8 = jnp.concatenate([ax] * 4, axis=0).astype(fp8)
    lead8 = jnp.concatenate([y8] * 4, axis=0).astype(fp8)
    return high, low, ax2, ax8, lead, lead8, xs, jnp.broadcast_to(weight * GAIN, (8, 128))


PIECES = 8
LIFT = 65536.0


def force_kernel(size, core, tiles_hbm, y8_hbm, force, own, other, tiles, y8, acc, meta, sems, entries, *buffers):
    load_meta = pltpu.make_async_copy(tiles_hbm.at[:, 2 * size, 0, :], meta, sems.at[0])
    load_tiles = pltpu.make_async_copy(tiles_hbm, tiles, sems.at[1])
    load_y8 = pltpu.make_async_copy(y8_hbm, y8, sems.at[2])
    load_meta.start()
    load_tiles.start()
    load_y8.start()
    acc[...] = jnp.zeros_like(acc)
    mine = core[0]
    load_meta.wait()

    def list_peer(peer, count):
        for half in range(2):
            base = (peer * 16) | (((half ^ mine) * MB) << 10)
            for c in range(size):
                spot = half * size + c
                block = meta[peer, spot].astype(jnp.int32)
                entries[count + c] = (base + spot) | (block << 10)
            count = count + meta[peer, 2 * size + half].astype(jnp.int32)
        return count

    total = lax.fori_loop(0, PEERS, list_peer, jnp.int32(0))
    last = entries[jnp.maximum(total - 1, 0)]
    for k in range(3 * GROUP):
        entries[total + k] = last | (1 << 20)
    trips = (total + 2 * GROUP - 1) // (2 * GROUP)
    load_tiles.wait()
    load_y8.wait()

    def unpack(index):
        entry = entries[index]
        return (entry >> 4) & 63, entry & 15, (entry >> 10) & 511, entry >> 20

    def stage_front(group, which):
        for u in range(GROUP):
            peer, c, block, extra = unpack(group * GROUP + u)
            keep = (1 - extra).astype(f32)
            base = (which * GROUP + u) * PIECES
            at = pl.ds(pl.multiple_of(block * 8, 8), 8)
            samples = jnp.concatenate([y8[0, at, :], y8[1, at, :]], axis=1)
            values = front(tiles[peer, c], samples, keep)
            for k in range(PIECES):
                buffers[base + k][...] = values[k]

    def stage_back(group, which):
        for u in range(GROUP):
            peer, c, block, extra = unpack(group * GROUP + u)
            base = (which * GROUP + u) * PIECES
            high, low, ax2, ax8, lead, lead8, xs, scale = [
                buffers[base + k][...] for k in range(PIECES)
            ]
            q = dot(ax2, high, 1, 0)
            f = dot(lead, high, 1, 1)
            q = q[0:8] + q[8:16] + dot(ax8, low, 1, 0)[0:8] * (1.0 / LIFT)
            f = f[0:8] + f[8:16] + dot(lead8, low, 1, 1)[0:8] * (1.0 / LIFT)
            f = scale * (xs * f[3:4] - f)
            force[peer, pl.ds(c * 3, 3), :] = f[0:3]
            at = pl.ds(pl.multiple_of(block * 8, 8), 8)
            for h in range(2):
                acc[h, at, :] = acc[h, at, :] + q[:, 128 * h : 128 * h + 128]

    stage_front(0, 0)

    def trip(i, unused):
        stage_front(2 * i + 1, 1)
        stage_back(2 * i, 0)
        stage_front(2 * i + 2, 0)
        stage_back(2 * i + 1, 1)
        return unused

    lax.fori_loop(0, trips, trip, 0)

    def finish(out, first):
        def one(i, unused):
            spot = (first + i * 8) * 8
            at = pl.ds(pl.multiple_of(i * 8, 8), 8)
            for h in range(2):
                amount = acc[h, pl.ds(spot + 4, 8, stride=8), :]
                for k in range(3):
                    rows = pl.ds(spot + k, 8, stride=8)
                    out[k, at, 128 * h : 128 * h + 128] = (y8[h, rows, :] * amount - acc[h, rows, :]) * GAIN
            return unused

        lax.fori_loop(0, MB // 8, one, 0, unroll=2)

    finish(own, 0)
    finish(other, MB)


def forces(size, core, tiles, y8):
    one = [
        pltpu.VMEM((QP, MP), bf16),
        pltpu.VMEM((QP, MP), fp8),
        pltpu.VMEM((16, QP), bf16),
        pltpu.VMEM((32, QP), fp8),
        pltpu.VMEM((16, MP), bf16),
        pltpu.VMEM((32, MP), fp8),
        pltpu.VMEM((8, QP), f32),
        pltpu.VMEM((8, QP), f32),
    ]
    part = jax.ShapeDtypeStruct((3, MB, MP), f32)
    return pl.pallas_call(
        functools.partial(force_kernel, size),
        name="forces",
        out_shape=(jax.ShapeDtypeStruct((PEERS, force_rows(size), QP), f32), part, part),
        in_specs=[SMEM_SPEC, ANY_SPEC, ANY_SPEC],
        out_specs=(VMEM_SPEC,) * 3,
        scratch_shapes=[
            pltpu.VMEM(tiles.shape, f32),
            pltpu.VMEM(y8.shape, f32),
            pltpu.VMEM(y8.shape, f32),
            pltpu.SMEM((PEERS, 128), f32),
            pltpu.SemaphoreType.DMA((3,)),
            pltpu.SMEM((2 * PEERS * size + CAP + 3 * GROUP,), jnp.int32),
        ]
        + one * (2 * GROUP),
    )(core, tiles, y8)


def force_rows(size):
    return -(-6 * size // 8) * 8


def gather_kernel(low, size, ps, cnt, force, out, even, odd):
    even[...] = jnp.zeros_like(even)
    odd[...] = jnp.zeros_like(odd)

    def one_peer(peer, unused):
        for half in range(2):
            owner = 2 * peer + half
            live = cnt[owner] - low
            for c in range(size):
                block = jnp.where(c < live, ps[owner * CAP + low + c], SB)
                row = 3 * (half * size + c)
                total = odd if (half * size + c) % 2 else even
                total[block] = total[block] + force[peer, row : row + 3, :]
        return unused

    lax.fori_loop(0, PEERS, one_peer, 0)
    out[...] = even[0:SB] + odd[0:SB]


def gather_forces(low, size, ps, cnt, force):
    return pl.pallas_call(
        functools.partial(gather_kernel, low, size),
        name="gather",
        out_shape=jax.ShapeDtypeStruct((SB, 3, QP), f32),
        in_specs=[SMEM_SPEC] * 2 + [VMEM_SPEC],
        out_specs=VMEM_SPEC,
        scratch_shapes=[pltpu.VMEM((SB + 1, 3, QP), f32)] * 2,
    )(ps, cnt, force)


def exchange(x):
    return lax.all_to_all(x, ("gx", "g"), split_axis=0, concat_axis=0, tiled=True)


def swap(x):
    return lax.ppermute(x, "core", [(0, 1), (1, 0)])


def spread_table():
    return jnp.kron(jnp.eye(16, dtype=f32), bezier_table())


def sums(blocks, table):
    lifted = jnp.concatenate([blocks[:3] * blocks[3:], blocks[3:]], axis=0)
    return jnp.einsum("cbk,jk->cbj", lifted, table, precision=lax.Precision.HIGHEST)


def body(slave_coords, slave_weight, master_ctrl, master_wt, pair_slave, pair_master, pair_count):
    coords = slave_coords.reshape(3, SB, QP).transpose(1, 0, 2)
    payload = pack(
        0, CAP, pair_slave, pair_master, pair_count, coords, slave_weight.reshape(SB, QP)
    )
    tiles = exchange(payload)

    blocks = jnp.concatenate([master_ctrl, master_wt[None, :]], axis=0).reshape(4, MB, MP)
    table = spread_table()
    own = sums(blocks, table)
    y8 = sample_tiles(own, sums(swap(blocks), table))

    core = lax.axis_index("core").reshape(1).astype(jnp.int32)
    force, q, away = forces(CAP, core, tiles, y8)
    slave_force = gather_forces(0, CAP, pair_slave, pair_count, exchange(force))

    q = (q + swap(away)) / own[3:]
    master_force = (
        jnp.einsum("cbj,jk->cbk", q, table, precision=lax.Precision.HIGHEST) * blocks[3:]
    )
    return (
        slave_force.transpose(1, 0, 2).reshape(3, SB * QP),
        master_force.reshape(3, MB * MP),
    )


def solution(mesh):
    split = Mesh(mesh.devices.reshape(4, 16, 2), ("gx", "g", "core"))
    every = ("gx", "g", "core")
    wide, flat = P(None, every), P(every)
    return jax.shard_map(
        body,
        mesh=split,
        in_specs=(wide, flat, wide, flat, flat, flat, flat),
        out_specs=(wide, wide),
        check_vma=False,
    )
```

time: 131 us -> 114 us (0.87); the launches traced: 131 us -> 113 us
  Pallas kernels: 22.7 us -> 46.4 us
  starting transfers between devices: 51.4 us -> 28.5 us
  other arithmetic: 18.2 us -> 3.72 us
  local copies, waits for them, and re-layouts: 20.3 us -> 7.37 us
  waiting for transfers between devices: 14.6 us -> 19.7 us
  matrix products: 2.85 us -> 6.09 us
    pallas_call x3 -> x4, Pallas kernels: 22.7 us -> 46.4 us  [the longest x1 30.9 us: forces(): pl.pallas_call(functools.partial(force_kernel, size), name='forces', out_...]
    all_to_all x2, starting transfers between devices: 51.3 us -> 28.4 us  [exchange(): lax.all_to_all(x, ('gx', 'g'), split_axis=0, concat_axis=0, tiled=True)]
    all_to_all x2, waiting for transfers between devices: 14.6 us -> 19.7 us  [exchange(): lax.all_to_all(x, ('gx', 'g'), split_axis=0, concat_axis=0, tiled=True)]
    unnamed x16 -> x21, local copies, waits for them, and re-layouts: 8.53 us -> 3.65 us
    mul x4 -> x2, other arithmetic: 6.99 us -> 2.29 us  [sums(): lifted = jnp.concatenate([blocks[:3] * blocks[3:], blocks[3:]], axis=0)]
    reduce_sum x2 -> x0, other arithmetic: 3.56 us -> none  [the longest x1 2.88 us: body(): norm = -0.5 * jnp.sum(scaled * scaled, axis=0, keepdims=True)]
    transpose x1 -> x0, other arithmetic: 3.33 us -> none  [body(): y8 = jnp.concatenate([scaled, jnp.ones_like(norm), norm, jnp.broadcast_to...]
    dot_general x2 -> x3, matrix products: 2.85 us -> 6.09 us  [the longest x2 5.29 us: sums(): jnp.einsum('cbk,jk->cbj', lifted, table, precision=lax.Precision.HIGHEST)]
  transfers between devices with their start and end apart: 4 -> 4, of which waited for: 2 -> 2; matrix products, arithmetic and copies ran while one was open for 20% -> 13% of each run, Pallas kernels for 3% -> 6%
where the time goes in v2:
time: 114 us; the launch traced here: 113 us
  Pallas kernels  46.4 us (41%)
  starting transfers between devices  28.5 us (25%)
  waiting for transfers between devices  19.7 us (17%)
  local copies, waits for them, and re-layouts  7.37 us (6%)
  matrix products  6.09 us (5%)
  other arithmetic  3.72 us (3%)
    pallas_call x1, Pallas kernels, forces(): pl.pallas_call(functools.partial(force_kernel, size), name='forces', out_...  30.9 us
    all_to_all x2, starting transfers between devices, exchange(): lax.all_to_all(x, ('gx', 'g'), split_axis=0, concat_axis=0, tiled=True)  28.4 us
    all_to_all x2, waiting for transfers between devices, exchange(): lax.all_to_all(x, ('gx', 'g'), split_axis=0, concat_axis=0, tiled=True)  19.7 us
    pallas_call x1, Pallas kernels, sample_tiles(): pl.pallas_call(sample_kernel, name='samples', out_shape=jax.ShapeDtypeStr...  6.96 us
    dot_general x2, matrix products, sums(): jnp.einsum('cbk,jk->cbj', lifted, table, precision=lax.Precision.HIGHEST)  5.29 us
    pallas_call x1, Pallas kernels, gather_forces(): pl.pallas_call(functools.partial(gather_kernel, low, size), name='gather'...  4.47 us
    pallas_call x1, Pallas kernels, pack(): pl.pallas_call(functools.partial(pack_kernel, low, size), name='pack', ou...  4.1 us
    unnamed x21, local copies, waits for them, and re-layouts  3.65 us
  transfers between devices with their start and end apart: 4, of which 2 were waited for; matrix products, arithmetic and copies ran while one was open for 13% of the time, Pallas kernels for 6%

profile of v2, /device:TPU:0, one launch (start us, length us, event | category | flops | bytes accessed | tf_op | source)
XLA Modules:
  0.0 112.6 jit_solution(843035520007456936)
XLA Ops:
  0.6 4.1 %pack.1 = f32[64,11,4,128]{3,2,1,0:T(4,128)} custom-call(s32[640]{0:T(1024)} %ps.3, s32[640]{0:T(1024)} %pm.1, s32[128]{0:T(128)} %cnt.3, f32[512,3,128]{2,1,0:T(4,128)} %bitcast.26, f32[512,128]{1,0:T(8,128)} %bitcast.28), custom_call_target="tpu_custom_call" | custom-call | tf_op jit(solution)/shard_map/pack/pallas_call | solution.py:74
  4.7 0.0 copy-start.4
  4.7 0.0 copy-start.5
  4.7 11.7 %all-to-all-start = ((f32[64,11,4,128]{3,2,1,0:T(4,128)}), f32[64,11,4,128]{3,2,1,0:T(4,128)S(1)}, u32[]{:S(2)}, u32[]{:S(2)}) async-start(f32[64,11,4,128]{3,2,1,0:T(4,128)} %pack.1), calls=%async_computation | async-start | bytes 2883584 | tf_op jit(solution)/shard_map/all_to_all | solution.py:308
  16.4 0.0 copy-done.4
  16.4 0.1 slice.21
  16.5 0.0 copy-start.3
  16.5 0.1 mul.97
  16.6 0.0 copy-start.6
  16.6 0.0 copy-done.5
  16.6 0.0 copy-start.8
  16.6 1.1 broadcast_multiply_fusion.1
  17.7 1.0 pad_maximum_fusion
  18.7 0.0 copy-done.3
  18.7 0.0 copy-done.6
  18.7 0.0 collective-permute-start
  18.8 0.0 copy-done.8
  18.8 0.1 power_multiply_fusion
  18.9 0.1 broadcast_multiply_fusion.2
  19.0 0.1 mul.107
  19.0 0.2 broadcast_multiply_fusion
  19.3 1.5 %reshape.192 = f32[256,256,1]{1,0,2:T(8,128)} reshape(f32[16,16,16,16]{3,2,1,0:T(8,128)S(1)} %broadcast_multiply_fusion) | data formatting | bytes 524288 | tf_op jit(solution)/shard_map/jit(kron)/mul | solution.py:316
  20.8 0.0 copy-start.2
  20.8 3.3 %fusion.1.own = f32[4,256,256]{2,1,0:T(8,128)} fusion(f32[256,256,1]{1,0,2:T(8,128)} %reshape.192, f32[1,256,256]{2,1,0:T(8,128)} %copy-done.3, f32[3,256,256]{2,1,0:T(8,128)} %get-tuple-element.8), kind=kOutput, calls=%fused_computation.4 | convolution fusion | flops 805568512 | bytes 2359296 | tf_op jit(solution)/shard_map/cbk,jk->cbj/dot_general | solution.py:321
  24.1 0.0 collective-permute-done
  24.1 1.0 slice_bitcast_fusion.1
  25.1 1.2 %slice_multiply_fusion = f32[3,256,256]{2,1,0:T(8,128)S(1)} fusion(f32[4,256,256]{2,1,0:T(8,128)} %collective-permute-done, f32[256,256]{1,0:T(8,128)S(1)} %get-tuple-element.10), kind=kLoop, calls=%fused_computation.12 | loop fusion | flops 196608 | bytes 1835008 | tf_op jit(solution)/shard_map/mul | solution.py:320
  26.3 0.0 copy-done.2
  26.3 2.0 %fusion.3.other = f32[4,256,256]{2,1,0:T(8,128)} fusion(f32[256,256,1]{1,0,2:T(8,128)S(1)} %copy-done.2, f32[1,256,256]{2,1,0:T(8,128)S(1)} %get-tuple-element.11, f32[3,256,256]{2,1,0:T(8,128)S(1)} %slice_multiply_fusion), kind=kOutput, calls=%fused_computation.6 | convolution fusion | flops 805568512 | bytes 2359296 | tf_op jit(solution)/shard_map/cbk,jk->cbj/dot_general | solution.py:321
  28.3 7.0 %samples.1.y8_hbm = f32[2,4096,128]{2,1,0:T(8,128)} custom-call(f32[4,256,256]{2,1,0:T(8,128)} %fusion.1.own, f32[4,256,256]{2,1,0:T(8,128)} %fusion.3.other), custom_call_target="tpu_custom_call" | custom-call | tf_op jit(solution)/shard_map/samples/pallas_call | solution.py:112
  35.2 3.9 %all-to-all-done.tiles_hbm = f32[64,11,4,128]{3,2,1,0:T(4,128)S(1)} async-done(((f32[64,11,4,128]{3,2,1,0:T(4,128)}), f32[64,11,4,128]{3,2,1,0:T(4,128)S(1)}, u32[]{:S(2)}, u32[]{:S(2)}) %all-to-all-start) | async-done | bytes 1441824 | tf_op jit(solution)/shard_map/all_to_all | solution.py:308
  39.2 0.0 copy-start
  39.2 1.1 %copy-done = f32[64,11,4,128]{3,2,1,0:T(4,128)} copy-done((f32[64,11,4,128]{3,2,1,0:T(4,128)}, f32[64,11,4,128]{3,2,1,0:T(4,128)S(1)}, u32[]{:S(2)}) %copy-start) | copy-done | bytes 1441816
  40.3 30.9 %forces.1 = (f32[64,32,128]{2,1,0:T(8,128)}, f32[3,256,256]{2,1,0:T(8,128)}, f32[3,256,256]{2,1,0:T(8,128)}) custom-call(s32[1]{0:T(128)} %bitcast.core, f32[64,11,4,128]{3,2,1,0:T(4,128)} %copy-done, f32[2,4096,128]{2,1,0:T(8,128)} %samples.1.y8_hbm), custom_call_target="tpu_custom_call" | custom-call | tf_op jit(solution)/shard_map/forces/pallas_call | solution.py:255
  71.3 0.0 copy-start.7
  71.3 0.0 copy-start.9
  71.3 0.1 collective-permute-start.1
  71.4 16.7 %all-to-all-start.1 = ((f32[64,32,128]{2,1,0:T(8,128)}), f32[64,32,128]{2,1,0:T(8,128)S(1)}, u32[]{:S(2)}, u32[]{:S(2)}) async-start(f32[64,32,128]{2,1,0:T(8,128)} %get-tuple-element.5), calls=%async_computation.1 | async-start | bytes 2097152 | tf_op jit(solution)/shard_map/all_to_all | solution.py:308
  88.1 1.0 slice_bitcast_fusion
  89.1 0.0 collective-permute-done.1
  89.1 0.0 copy-done.7
  89.1 0.0 copy-done.9
  89.1 0.8 fusion
  89.9 1.5 %copy.11 = f32[1,3,256,256]{3,1,2,0:T(4,128)} copy(f32[1,3,256,256]{3,2,1,0:T(8,128)S(1)} %fusion) | data formatting | bytes 1572864
  91.4 15.7 %all-to-all-done.1.force = f32[64,32,128]{2,1,0:T(8,128)S(1)} async-done(((f32[64,32,128]{2,1,0:T(8,128)}), f32[64,32,128]{2,1,0:T(8,128)S(1)}, u32[]{:S(2)}, u32[]{:S(2)}) %all-to-all-start.1) | async-done | bytes 1048608 | tf_op jit(solution)/shard_map/all_to_all | solution.py:308
  107.2 0.0 copy-start.1
  107.2 1.0 copy-done.1
  108.1 4.5 %gather.1 = f32[512,3,128]{2,1,0:T(4,128)} custom-call(s32[640]{0:T(1024)} %ps.3, s32[128]{0:T(128)} %cnt.3, f32[64,32,128]{2,1,0:T(8,128)} %copy-done.1), custom_call_target="tpu_custom_call" | custom-call | tf_op jit(solution)/shard_map/gather/pallas_call | solution.py:297
  (3 shorter events, 0.0 us)
Async XLA Ops:
  4.7 11.7 %copy-start.4 = (f32[65536]{0:T(1024)S(1)}, f32[65536]{0:T(1024)}, u32[]{:S(2)}) copy-start(f32[65536]{0:T(1024)} %param.11) | copy-start | bytes 786436
  4.7 11.9 %copy-start.5 = (f32[3,65536]{1,0:T(4,128)S(1)}, f32[3,65536]{1,0:T(4,128)}, u32[]{:S(2)}) copy-start(f32[3,65536]{1,0:T(4,128)} %param.10) | copy-start | bytes 2359300
  4.7 34.5 %all-to-all-start = ((f32[64,11,4,128]{3,2,1,0:T(4,128)}), f32[64,11,4,128]{3,2,1,0:T(4,128)S(1)}, u32[]{:S(2)}, u32[]{:S(2)}) async-start(f32[64,11,4,128]{3,2,1,0:T(4,128)} %pack.1), calls=%async_computation | async-start | bytes 2883584 | tf_op jit(solution)/shard_map/all_to_all | solution.py:308
  16.5 2.2 %copy-start.3 = (f32[1,256,256]{2,1,0:T(8,128)}, f32[1,256,256]{2,1,0:T(8,128)S(1)}, u32[]{:S(2)}) copy-start(f32[1,256,256]{2,1,0:T(8,128)S(1)} %slice.21) | copy-start | bytes 786436
  16.6 2.2 %copy-start.6 = (f32[256,256]{1,0:T(8,128)}, f32[256,256]{1,0:T(8,128)S(1)}, u32[]{:S(2)}) copy-start(f32[256,256]{1,0:T(8,128)S(1)} %mul.97) | copy-start | bytes 786436
  16.6 2.2 %copy-start.8 = (f32[4]{0:T(128)S(1)}, f32[4]{0:T(128)}, u32[]{:S(2)}) copy-start(f32[4]{0:T(128)} %constant.15.clone) | copy-start | bytes 52
  18.7 5.3 %collective-permute-start = (f32[4,256,256]{2,1,0:T(8,128)}, f32[4,256,256]{2,1,0:T(8,128)}, u32[]{:S(2)}, u32[]{:S(2)}) collective-permute-start(f32[4,256,256]{2,1,0:T(8,128)} %pad_maximum_fusion), channel_id=1, source_target_pairs={{0,1},{1,0},{2,3},{3,2},{4,5},{5,4},{6,7},{7,6},{8,9},{9,8},{10,11... | collective-permute-start | bytes 3145736 | tf_op jit(solution)/shard_map/ppermute | solution.py:312
  20.8 5.5 %copy-start.2 = (f32[256,256,1]{1,0,2:T(8,128)S(1)}, f32[256,256,1]{1,0,2:T(8,128)}, u32[]{:S(2)}) copy-start(f32[256,256,1]{1,0,2:T(8,128)} %reshape.192) | copy-start | bytes 786436
  39.2 1.1 %copy-start = (f32[64,11,4,128]{3,2,1,0:T(4,128)}, f32[64,11,4,128]{3,2,1,0:T(4,128)S(1)}, u32[]{:S(2)}) copy-start(f32[64,11,4,128]{3,2,1,0:T(4,128)S(1)} %all-to-all-done.tiles_hbm) | copy-start | bytes 4325380
  71.3 17.9 %copy-start.7 = (f32[256,256]{1,0:T(8,128)S(1)}, f32[256,256]{1,0:T(8,128)}, u32[]{:S(2)}) copy-start(f32[256,256]{1,0:T(8,128)} %copy-done.6) | copy-start | bytes 786436
  71.3 17.9 %copy-start.9 = (f32[3,256,256]{2,1,0:T(8,128)S(1)}, f32[3,256,256]{2,1,0:T(8,128)}, u32[]{:S(2)}) copy-start(f32[3,256,256]{2,1,0:T(8,128)} %get-tuple-element.6) | copy-start | bytes 2359300
  71.3 17.8 %collective-permute-start.1 = (f32[3,256,256]{2,1,0:T(8,128)}, f32[3,256,256]{2,1,0:T(8,128)S(1)}, u32[]{:S(2)}, u32[]{:S(2)}) collective-permute-start(f32[3,256,256]{2,1,0:T(8,128)} %get-tuple-element.7), channel_id=1, source_target_pairs={{0,1},{1,0},{2,3},{3,2},{4,5},{5,4},{6,7},{7,6},{8,9},{9,8},{10,11... | collective-permute-start | bytes 2359304 | tf_op jit(solution)/shard_map/ppermute | solution.py:312
  71.4 35.8 %all-to-all-start.1 = ((f32[64,32,128]{2,1,0:T(8,128)}), f32[64,32,128]{2,1,0:T(8,128)S(1)}, u32[]{:S(2)}, u32[]{:S(2)}) async-start(f32[64,32,128]{2,1,0:T(8,128)} %get-tuple-element.5), calls=%async_computation.1 | async-start | bytes 2097152 | tf_op jit(solution)/shard_map/all_to_all | solution.py:308
  107.2 1.0 copy-start.1

commit v3 on v2

--- a/solution.py
+++ b/solution.py
@@ -3,11 +3,13 @@
 
 import jax
 import jax.numpy as jnp
+import numpy as np
 from jax import lax
 from jax.experimental import pallas as pl
 from jax.experimental.pallas import tpu as pltpu
 from jax.sharding import Mesh
 from jax.sharding import PartitionSpec as P
+
 
 QP = 128
 CAP = 5
@@ -15,7 +17,7 @@
 MB = 256
 MP = 256
 PEERS = 64
-GROUP = 4
+GROUP = 8
 
 f32 = jnp.float32
 bf16 = jnp.bfloat16
@@ -29,15 +31,19 @@
 
 
 def bezier_table():
-    params = (jnp.arange(4, dtype=f32) + 0.5) / 4.0
-    powers = jnp.arange(4, dtype=f32)
-    binomial = jnp.array([1.0, 3.0, 3.0, 1.0], dtype=f32)
+    params = (np.arange(4) + 0.5) / 4.0
+    powers = np.arange(4)
+    binomial = np.array([1.0, 3.0, 3.0, 1.0])
     bernstein = (
         binomial[None, :]
         * params[:, None] ** powers[None, :]
         * (1.0 - params[:, None]) ** (3.0 - powers[None, :])
     )
     return (bernstein[:, None, :, None] * bernstein[None, :, None, :]).reshape(16, 16)
+
+
+def spread_table():
+    return jnp.asarray(np.kron(np.eye(16), bezier_table()).astype(np.float32))
 
 
 def dot(a, b, left, right):
@@ -80,15 +86,30 @@
     )(ps, pm, cnt, coords, weight)
 
 
-def sample_kernel(own, other, y8):
-    def eight(source, base):
+def sample_kernel(own, other, table, y8, total, sums):
+    def halves(source, base):
+        def lift(k, unused):
+            rows = source[k] * jnp.where(k == 3, 1.0, source[3])
+            sums[k] = lax.dot_general(
+                rows,
+                table[...],
+                (((1,), (1,)), ((), ())),
+                precision=lax.Precision.HIGHEST,
+                preferred_element_type=f32,
+            )
+            return unused
+
+        lax.fori_loop(0, 4, lift, 0)
+        if base == 0:
+            total[...] = sums[3]
+
         def one(i, unused):
             at = pl.ds(pl.multiple_of(i * 8, 8), 8)
-            inverse = 1.0 / source[3, at, :]
+            inverse = 1.0 / sums[3, at, :]
             norm = jnp.zeros((8, MP), f32)
             spot = (base + i * 8) * 8
             for k in range(3):
-                y = source[k, at, :] * inverse
+                y = sums[k, at, :] * inverse
                 centre = jnp.sum(y, axis=1, keepdims=True) * (1.0 / MP)
                 y = (y - centre) * SCALE
                 norm = norm - 0.5 * (y * y)
@@ -102,20 +123,24 @@
                 y8[h, pl.ds(spot + 4, 8, stride=8), :] = norm[:, lanes]
             return unused
 
-        lax.fori_loop(0, MB // 8, one, 0, unroll=2)
-
-    eight(own, 0)
-    eight(other, MB)
-
-
-def sample_tiles(own, other):
+        lax.fori_loop(0, MB // 8, one, 0, unroll=4)
+
+    halves(own, 0)
+    halves(other, MB)
+
+
+def sample_tiles(own, other, table):
     return pl.pallas_call(
         sample_kernel,
         name="samples",
-        out_shape=jax.ShapeDtypeStruct((2, 2 * MB * 8, 128), f32),
-        in_specs=[VMEM_SPEC] * 2,
-        out_specs=VMEM_SPEC,
-    )(own, other)
+        out_shape=(
+            jax.ShapeDtypeStruct((2, 2 * MB * 8, 128), f32),
+            jax.ShapeDtypeStruct((MB, MP), f32),
+        ),
+        in_specs=[VMEM_SPEC] * 3,
+        out_specs=(VMEM_SPEC,) * 2,
+        scratch_shapes=[pltpu.VMEM((4, MB, MP), f32)],
+    )(own, other, table)
 
 
 def front(tile, y8, keep):
@@ -151,12 +176,10 @@
 LIFT = 65536.0
 
 
-def force_kernel(size, core, tiles_hbm, y8_hbm, force, own, other, tiles, y8, acc, meta, sems, entries, *buffers):
-    load_meta = pltpu.make_async_copy(tiles_hbm.at[:, 2 * size, 0, :], meta, sems.at[0])
-    load_tiles = pltpu.make_async_copy(tiles_hbm, tiles, sems.at[1])
-    load_y8 = pltpu.make_async_copy(y8_hbm, y8, sems.at[2])
+def force_kernel(size, core, tiles, y8_hbm, force, own, other, y8, acc, meta, sems, entries, *buffers):
+    load_meta = pltpu.make_async_copy(tiles.at[:, 2 * size, 0, :], meta, sems.at[0])
     load_meta.start()
-    load_tiles.start()
+    load_y8 = pltpu.make_async_copy(y8_hbm, y8, sems.at[1])
     load_y8.start()
     acc[...] = jnp.zeros_like(acc)
     mine = core[0]
@@ -177,7 +200,7 @@
     for k in range(3 * GROUP):
         entries[total + k] = last | (1 << 20)
     trips = (total + 2 * GROUP - 1) // (2 * GROUP)
-    load_tiles.wait()
+
     load_y8.wait()
 
     def unpack(index):
@@ -197,7 +220,7 @@
 
     def stage_back(group, which):
         for u in range(GROUP):
-            peer, c, block, extra = unpack(group * GROUP + u)
+            peer, c, block, _ = unpack(group * GROUP + u)
             base = (which * GROUP + u) * PIECES
             high, low, ax2, ax8, lead, lead8, xs, scale = [
                 buffers[base + k][...] for k in range(PIECES)
@@ -234,7 +257,7 @@
                     out[k, at, 128 * h : 128 * h + 128] = (y8[h, rows, :] * amount - acc[h, rows, :]) * GAIN
             return unused
 
-        lax.fori_loop(0, MB // 8, one, 0, unroll=2)
+        lax.fori_loop(0, MB // 8, one, 0, unroll=4)
 
     finish(own, 0)
     finish(other, MB)
@@ -256,14 +279,13 @@
         functools.partial(force_kernel, size),
         name="forces",
         out_shape=(jax.ShapeDtypeStruct((PEERS, force_rows(size), QP), f32), part, part),
-        in_specs=[SMEM_SPEC, ANY_SPEC, ANY_SPEC],
+        in_specs=[SMEM_SPEC, VMEM_SPEC, ANY_SPEC],
         out_specs=(VMEM_SPEC,) * 3,
         scratch_shapes=[
-            pltpu.VMEM(tiles.shape, f32),
             pltpu.VMEM(y8.shape, f32),
             pltpu.VMEM(y8.shape, f32),
             pltpu.SMEM((PEERS, 128), f32),
-            pltpu.SemaphoreType.DMA((3,)),
+            pltpu.SemaphoreType.DMA((2,)),
             pltpu.SMEM((2 * PEERS * size + CAP + 3 * GROUP,), jnp.int32),
         ]
         + one * (2 * GROUP),
@@ -312,15 +334,6 @@
     return lax.ppermute(x, "core", [(0, 1), (1, 0)])
 
 
-def spread_table():
-    return jnp.kron(jnp.eye(16, dtype=f32), bezier_table())
-
-
-def sums(blocks, table):
-    lifted = jnp.concatenate([blocks[:3] * blocks[3:], blocks[3:]], axis=0)
-    return jnp.einsum("cbk,jk->cbj", lifted, table, precision=lax.Precision.HIGHEST)
-
-
 def body(slave_coords, slave_weight, master_ctrl, master_wt, pair_slave, pair_master, pair_count):
     coords = slave_coords.reshape(3, SB, QP).transpose(1, 0, 2)
     payload = pack(
@@ -330,14 +343,18 @@
 
     blocks = jnp.concatenate([master_ctrl, master_wt[None, :]], axis=0).reshape(4, MB, MP)
     table = spread_table()
-    own = sums(blocks, table)
-    y8 = sample_tiles(own, sums(swap(blocks), table))
+    y8, total = sample_tiles(blocks, swap(blocks), table)
 
     core = lax.axis_index("core").reshape(1).astype(jnp.int32)
+    tiles = pltpu.with_memory_space_constraint(tiles, pltpu.VMEM)
     force, q, away = forces(CAP, core, tiles, y8)
-    slave_force = gather_forces(0, CAP, pair_slave, pair_count, exchange(force))
-
-    q = (q + swap(away)) / own[3:]
+    force = exchange(force)
+    away = swap(away)
+    slave_force = gather_forces(
+        0, CAP, pair_slave, pair_count, pltpu.with_memory_space_constraint(force, pltpu.VMEM)
+    )
+
+    q = (q + away) / total
     master_force = (
         jnp.einsum("cbj,jk->cbk", q, table, precision=lax.Precision.HIGHEST) * blocks[3:]
     )

time: 114 us -> 107 us (0.939)
  waiting for transfers between devices: 19.7 us -> 26.9 us
  starting transfers between devices: 28.5 us -> 23.3 us
  matrix products: 6.09 us -> 1.75 us
  other arithmetic: 3.72 us -> 0 us
  local copies, waits for them, and re-layouts: 7.37 us -> 4.32 us
  Pallas kernels: 46.4 us -> 49 us
    all_to_all x2, starting transfers between devices: 28.4 us -> 23.1 us  [exchange(): lax.all_to_all(x, ('gx', 'g'), split_axis=0, concat_axis=0, tiled=True)]
    dot_general x2 -> x0, matrix products: 5.29 us -> none  [sums(): jnp.einsum('cbk,jk->cbj', lifted, table, precision=lax.Precision.HIGHEST)]
    all_to_all x2, waiting for transfers between devices: 19.7 us -> 24.3 us  [exchange(): lax.all_to_all(x, ('gx', 'g'), split_axis=0, concat_axis=0, tiled=True)]
    mul x5 -> x0, other arithmetic: 2.66 us -> none  [the longest x2 2.29 us: sums(): lifted = jnp.concatenate([blocks[:3] * blocks[3:], blocks[3:]], axis=0)]
    ppermute x2, waiting for transfers between devices: 0.01 us -> 2.65 us  [swap(): return lax.ppermute(x, 'core', [(0, 1), (1, 0)])]
    mul x4 -> x1, local copies, waits for them, and re-layouts: 2.67 us -> 0.07 us  [body(): jnp.einsum('cbj,jk->cbk', q, table, precision=lax.Precision.HIGHEST)]
    pallas_call x1, Pallas kernels: 6.96 us -> 8.88 us  [sample_tiles(): pl.pallas_call(sample_kernel, name='samples', out_shape=(jax.ShapeDtypeSt...]
    pallas_call x1, Pallas kernels: 30.9 us -> 32.1 us  [forces(): pl.pallas_call(functools.partial(force_kernel, size), name='forces', out_...]
  transfers between devices with their start and end apart: 4 -> 4, of which waited for: 2 -> 3; matrix products, arithmetic and copies ran while one was open for 13% -> 4% of each run, Pallas kernels for 6% -> 8%
where the time goes in v3:
time: 107 us; the launch traced here: 106 us
  Pallas kernels  49 us (46%)
  waiting for transfers between devices  26.9 us (25%)
  starting transfers between devices  23.3 us (22%)
  local copies, waits for them, and re-layouts  4.32 us (4%)
  matrix products  1.75 us (2%)
    pallas_call x1, Pallas kernels, forces(): pl.pallas_call(functools.partial(force_kernel, size), name='forces', out_...  32.1 us
    all_to_all x2, waiting for transfers between devices, exchange(): lax.all_to_all(x, ('gx', 'g'), split_axis=0, concat_axis=0, tiled=True)  24.3 us
    all_to_all x2, starting transfers between devices, exchange(): lax.all_to_all(x, ('gx', 'g'), split_axis=0, concat_axis=0, tiled=True)  23.1 us
    pallas_call x1, Pallas kernels, sample_tiles(): pl.pallas_call(sample_kernel, name='samples', out_shape=(jax.ShapeDtypeSt...  8.88 us
    pallas_call x1, Pallas kernels, pack(): pl.pallas_call(functools.partial(pack_kernel, low, size), name='pack', ou...  4.1 us
    pallas_call x1, Pallas kernels, gather_forces(): pl.pallas_call(functools.partial(gather_kernel, low, size), name='gather'...  3.94 us
    unnamed x18, local copies, waits for them, and re-layouts  3.45 us
    ppermute x2, waiting for transfers between devices, swap(): return lax.ppermute(x, 'core', [(0, 1), (1, 0)])  2.65 us
  transfers between devices with their start and end apart: 4, of which 3 were waited for; matrix products, arithmetic and copies ran while one was open for 4% of the time, Pallas kernels for 8%

profile of v3, /device:TPU:0, one launch (start us, length us, event | category | flops | bytes accessed | tf_op | source)
XLA Modules:
  0.0 106.1 jit_solution(11909869671361714723)
XLA Ops:
  0.6 4.1 %pack.1 = f32[64,11,4,128]{3,2,1,0:T(4,128)} custom-call(s32[640]{0:T(1024)} %ps.3, s32[640]{0:T(1024)} %pm.1, s32[128]{0:T(128)} %cnt.3, f32[512,3,128]{2,1,0:T(4,128)} %bitcast.19, f32[512,128]{1,0:T(8,128)} %bitcast.20), custom_call_target="tpu_custom_call" | custom-call | tf_op jit(solution)/shard_map/pack/pallas_call | solution.py:80
  4.7 0.0 copy-start.3
  4.7 0.0 copy-start.1
  4.7 11.7 %all-to-all-start = ((f32[64,11,4,128]{3,2,1,0:T(4,128)}), f32[64,11,4,128]{3,2,1,0:T(4,128)S(1)}, u32[]{:S(2)}, u32[]{:S(2)}) async-start(f32[64,11,4,128]{3,2,1,0:T(4,128)} %pack.1), calls=%async_computation | async-start | bytes 2883584 | tf_op jit(solution)/shard_map/all_to_all | solution.py:330
  16.4 0.0 copy-done.3
  16.4 0.8 concatenate.9
  17.2 0.0 copy-start.5
  17.2 0.0 copy-done.1
  17.2 0.2 bitcast_dynamic-update-slice_fusion
  17.3 0.8 copy-done.5
  18.2 0.0 copy-start
  18.2 0.1 collective-permute-start
  18.3 2.6 %collective-permute-done.other = f32[4,256,256]{2,1,0:T(8,128)S(1)} collective-permute-done((f32[4,256,256]{2,1,0:T(8,128)S(1)}, f32[4,256,256]{2,1,0:T(8,128)S(1)}, u32[]{:S(2)}, u32[]{:S(2)}) %collective-permute-start) | collective-permute-done | bytes 1048608 | tf_op jit(solution)/shard_map/ppermute | solution.py:334
  20.9 0.0 copy-done
  20.9 0.0 copy-start.2
  20.9 1.0 copy-done.2
  21.9 8.9 %samples.1 = (f32[2,4096,128]{2,1,0:T(8,128)}, f32[256,256]{1,0:T(8,128)}) custom-call(f32[4,256,256]{2,1,0:T(8,128)} %copy-done, f32[4,256,256]{2,1,0:T(8,128)} %copy-done.2, f32[256,256]{1,0:T(8,128)} %constant.6.clone.table), custom_call_target="tpu_custom_call" | custom-call | tf_op jit(solution)/shard_map/samples/pallas_call | solution.py:133
  30.8 8.4 %all-to-all-done.tiles = f32[64,11,4,128]{3,2,1,0:T(4,128)S(1)} async-done(((f32[64,11,4,128]{3,2,1,0:T(4,128)}), f32[64,11,4,128]{3,2,1,0:T(4,128)S(1)}, u32[]{:S(2)}, u32[]{:S(2)}) %all-to-all-start) | async-done | bytes 1441824 | tf_op jit(solution)/shard_map/all_to_all | solution.py:330
  39.2 32.1 %forces.1 = (f32[64,32,128]{2,1,0:T(8,128)}, f32[3,256,256]{2,1,0:T(8,128)}, f32[3,256,256]{2,1,0:T(8,128)}) custom-call(s32[1]{0:T(128)} %bitcast.core, f32[64,11,4,128]{3,2,1,0:T(4,128)S(1)} %all-to-all-done.tiles, f32[2,4096,128]{2,1,0:T(8,128)} %get-tuple-element.7.y8_hbm), custom_call_target="tpu_custom_call" | custom-call | tf_op jit(solution)/shard_map/forces/pallas_call | solution.py:278
  71.3 0.0 copy-start.4
  71.3 0.0 copy-start.6
  71.3 0.0 copy-start.7
  71.3 0.1 collective-permute-start.1
  71.4 11.5 %all-to-all-start.1 = ((f32[64,32,128]{2,1,0:T(8,128)}), f32[64,32,128]{2,1,0:T(8,128)S(1)}, u32[]{:S(2)}, u32[]{:S(2)}) async-start(f32[64,32,128]{2,1,0:T(8,128)} %get-tuple-element.8), calls=%async_computation.1 | async-start | bytes 2097152 | tf_op jit(solution)/shard_map/all_to_all | solution.py:330
  82.9 0.0 copy-done.4
  82.9 0.1 mul.10
  83.0 0.0 collective-permute-done.1
  83.0 0.0 copy-done.6
  83.0 0.0 copy-done.7
  83.0 1.8 %fusion = f32[1,3,256,256]{3,2,1,0:T(8,128)S(1)} fusion(f32[256,256,1]{1,0,2:T(8,128)} %constant.7, f32[3,256,256]{2,1,0:T(8,128)S(1)} %copy-done.6, f32[3,256,256]{2,1,0:T(8,128)S(1)} %collective-permute-done.1, f32[256,256]{1,0:T(8,128)S(1)} %mul.10, f32[256,256]{1,0:T(8,128)S(1)} %copy-done.7), kind=kOutput, calls=%fused_computation.1 | convolution fusion | flops 604569600 | bytes 3145728 | tf_op jit(solution)/shard_map/cbj,jk->cbk/dot_general | solution.py:359
  84.8 1.5 %copy.11 = f32[1,3,256,256]{3,1,2,0:T(4,128)} copy(f32[1,3,256,256]{3,2,1,0:T(8,128)S(1)} %fusion) | data formatting | bytes 1572864
  86.3 15.8 %all-to-all-done.1.force = f32[64,32,128]{2,1,0:T(8,128)S(1)} async-done(((f32[64,32,128]{2,1,0:T(8,128)}), f32[64,32,128]{2,1,0:T(8,128)S(1)}, u32[]{:S(2)}, u32[]{:S(2)}) %all-to-all-start.1) | async-done | bytes 1048608 | tf_op jit(solution)/shard_map/all_to_all | solution.py:330
  102.1 3.9 %gather.1 = f32[512,3,128]{2,1,0:T(4,128)} custom-call(s32[640]{0:T(1024)} %ps.3, s32[128]{0:T(128)} %cnt.3, f32[64,32,128]{2,1,0:T(8,128)S(1)} %all-to-all-done.1.force), custom_call_target="tpu_custom_call" | custom-call | tf_op jit(solution)/shard_map/gather/pallas_call | solution.py:319
  (1 shorter events, 0.0 us)
Async XLA Ops:
  4.7 11.7 %copy-start.3 = (f32[65536]{0:T(1024)S(1)}, f32[65536]{0:T(1024)}, u32[]{:S(2)}) copy-start(f32[65536]{0:T(1024)} %param.11) | copy-start | bytes 786436
  4.7 12.5 %copy-start.1 = (f32[3,65536]{1,0:T(4,128)S(1)}, f32[3,65536]{1,0:T(4,128)}, u32[]{:S(2)}) copy-start(f32[3,65536]{1,0:T(4,128)} %param.10) | copy-start | bytes 2359300
  4.7 34.5 %all-to-all-start = ((f32[64,11,4,128]{3,2,1,0:T(4,128)}), f32[64,11,4,128]{3,2,1,0:T(4,128)S(1)}, u32[]{:S(2)}, u32[]{:S(2)}) async-start(f32[64,11,4,128]{3,2,1,0:T(4,128)} %pack.1), calls=%async_computation | async-start | bytes 2883584 | tf_op jit(solution)/shard_map/all_to_all | solution.py:330
  17.2 0.9 copy-start.5
  18.2 2.8 %copy-start = (f32[4,256,256]{2,1,0:T(8,128)}, f32[4,256,256]{2,1,0:T(8,128)S(1)}, u32[]{:S(2)}) copy-start(f32[4,256,256]{2,1,0:T(8,128)S(1)} %constant_dynamic-update-slice_fusion.own) | copy-start | bytes 3145732
  18.2 2.7 %collective-permute-start = (f32[4,256,256]{2,1,0:T(8,128)S(1)}, f32[4,256,256]{2,1,0:T(8,128)S(1)}, u32[]{:S(2)}, u32[]{:S(2)}) collective-permute-start(f32[4,256,256]{2,1,0:T(8,128)S(1)} %constant_dynamic-update-slice_fusion.own), channel_id=1, source_target_pairs={{0,1},{1,0},{2,3},{3,2},{4,5},{5,4},{6,7},{7,6},{8,9},{9,8},{10,11... | collective-permute-start | bytes 3145736 | tf_op jit(solution)/shard_map/ppermute | solution.py:334
  20.9 1.0 copy-start.2
  71.3 11.6 %copy-start.4 = (f32[65536]{0:T(1024)S(1)}, f32[65536]{0:T(1024)}, u32[]{:S(2)}) copy-start(f32[65536]{0:T(1024)} %param.11) | copy-start | bytes 786436
  71.3 11.7 %copy-start.6 = (f32[3,256,256]{2,1,0:T(8,128)S(1)}, f32[3,256,256]{2,1,0:T(8,128)}, u32[]{:S(2)}) copy-start(f32[3,256,256]{2,1,0:T(8,128)} %get-tuple-element.9) | copy-start | bytes 2359300
  71.3 11.7 %copy-start.7 = (f32[256,256]{1,0:T(8,128)S(1)}, f32[256,256]{1,0:T(8,128)}, u32[]{:S(2)}) copy-start(f32[256,256]{1,0:T(8,128)} %get-tuple-element.11) | copy-start | bytes 786436
  71.3 11.7 %collective-permute-start.1 = (f32[3,256,256]{2,1,0:T(8,128)}, f32[3,256,256]{2,1,0:T(8,128)S(1)}, u32[]{:S(2)}, u32[]{:S(2)}) collective-permute-start(f32[3,256,256]{2,1,0:T(8,128)} %get-tuple-element.10), channel_id=1, source_target_pairs={{0,1},{1,0},{2,3},{3,2},{4,5},{5,4},{6,7},{7,6},{8,9},{9,8},{10,11... | collective-permute-start | bytes 2359304 | tf_op jit(solution)/shard_map/ppermute | solution.py:334
  71.4 30.7 %all-to-all-start.1 = ((f32[64,32,128]{2,1,0:T(8,128)}), f32[64,32,128]{2,1,0:T(8,128)S(1)}, u32[]{:S(2)}, u32[]{:S(2)}) async-start(f32[64,32,128]{2,1,0:T(8,128)} %get-tuple-element.8), calls=%async_computation.1 | async-start | bytes 2097152 | tf_op jit(solution)/shard_map/all_to_all | solution.py:330

commit v4 on v3

--- a/solution.py
+++ b/solution.py
@@ -54,35 +54,45 @@
     return x.astype(bf16).astype(f32)
 
 
-def pack_kernel(low, size, ps, pm, cnt, coords, weight, out):
+def pack_kernel(size, ps, pm, cnt, coords, weight, out, built, sems):
     lane = lax.broadcasted_iota(jnp.int32, (1, 128), 1)
+    share = PEERS // PARTS
 
     def one_peer(peer, unused):
         row = jnp.zeros((1, 128), jnp.int32)
-        for half in range(2):
-            owner = 2 * peer + half
-            for c in range(size):
-                slot = owner * CAP + low + c
-                block = ps[slot]
-                spot = half * size + c
-                out[peer, spot, 0:3, :] = coords[block]
-                out[peer, spot, 3:4, :] = weight[pl.ds(block, 1), :]
-                row = jnp.where(lane == spot, pm[slot], row)
-            live = jnp.clip(cnt[owner] - low, 0, size)
-            row = jnp.where(lane == 2 * size + half, live, row)
-        out[peer, 2 * size, 0:1, :] = row.astype(f32)
+        for spot in range(2 * size):
+            slot = peer * (2 * size) + spot
+            block = ps[slot]
+            built[peer, spot, 0:3, :] = coords[block]
+            built[peer, spot, 3:4, :] = weight[pl.ds(block, 1), :]
+            row = jnp.where(lane == spot, pm[slot], row)
+        for owner in range(2):
+            row = jnp.where(lane == 2 * size + owner, cnt[2 * peer + owner], row)
+        built[peer, 2 * size, 0:1, :] = row.astype(f32)
         return unused
 
-    lax.fori_loop(0, PEERS, one_peer, 0)
-
-
-def pack(low, size, ps, pm, cnt, coords, weight):
+    copies = []
+    for part in range(PARTS):
+        lax.fori_loop(part * share, (part + 1) * share, one_peer, 0, unroll=2)
+        some = pl.ds(part * share, share)
+        copies.append(pltpu.make_async_copy(built.at[some], out.at[some], sems.at[part]))
+        copies[-1].start()
+    for copy in copies:
+        copy.wait()
+
+
+PARTS = 4
+
+
+def pack(size, ps, pm, cnt, coords, weight):
+    shape = (PEERS, 2 * size + 1, 4, QP)
     return pl.pallas_call(
-        functools.partial(pack_kernel, low, size),
+        functools.partial(pack_kernel, size),
         name="pack",
-        out_shape=jax.ShapeDtypeStruct((PEERS, 2 * size + 1, 4, QP), f32),
+        out_shape=jax.ShapeDtypeStruct(shape, f32),
         in_specs=[SMEM_SPEC] * 3 + [VMEM_SPEC] * 2,
-        out_specs=VMEM_SPEC,
+        out_specs=ANY_SPEC,
+        scratch_shapes=[pltpu.VMEM(shape, f32), pltpu.SemaphoreType.DMA((PARTS,))],
     )(ps, pm, cnt, coords, weight)
 
 
@@ -176,26 +186,36 @@
 LIFT = 65536.0
 
 
-def force_kernel(size, core, tiles, y8_hbm, force, own, other, y8, acc, meta, sems, entries, *buffers):
-    load_meta = pltpu.make_async_copy(tiles.at[:, 2 * size, 0, :], meta, sems.at[0])
-    load_meta.start()
+def force_kernel(size, core, tiles, y8_hbm, force, own, other, y8, acc, rows, meta, sems, entries, *buffers):
     load_y8 = pltpu.make_async_copy(y8_hbm, y8, sems.at[1])
     load_y8.start()
+
+    def row_of(peer, unused):
+        rows[pl.ds(peer, 1), :] = tiles[peer, 2 * size, 0:1, :].astype(jnp.int32)
+        return unused
+
+    lax.fori_loop(0, PEERS, row_of, 0, unroll=8)
+    lane = lax.broadcasted_iota(jnp.int32, (PEERS, 128), 1)
+    chip = lax.broadcasted_iota(jnp.int32, (PEERS, 128), 0)
+    mine = core[0]
+    half = jnp.where(lane < size, mine, 1 - mine)
+    sent = rows[...]
+    rows[...] = jnp.where(
+        lane < 2 * size, (half * MB + sent) * 1024 + chip * 16 + lane, sent
+    )
+    load_meta = pltpu.make_async_copy(rows, meta, sems.at[0])
+    load_meta.start()
     acc[...] = jnp.zeros_like(acc)
-    mine = core[0]
     load_meta.wait()
 
     def list_peer(peer, count):
         for half in range(2):
-            base = (peer * 16) | (((half ^ mine) * MB) << 10)
             for c in range(size):
-                spot = half * size + c
-                block = meta[peer, spot].astype(jnp.int32)
-                entries[count + c] = (base + spot) | (block << 10)
-            count = count + meta[peer, 2 * size + half].astype(jnp.int32)
+                entries[count + c] = meta[peer, half * size + c]
+            count = count + meta[peer, 2 * size + half]
         return count
 
-    total = lax.fori_loop(0, PEERS, list_peer, jnp.int32(0))
+    total = lax.fori_loop(0, PEERS, list_peer, jnp.int32(0), unroll=2)
     last = entries[jnp.maximum(total - 1, 0)]
     for k in range(3 * GROUP):
         entries[total + k] = last | (1 << 20)
@@ -284,7 +304,8 @@
         scratch_shapes=[
             pltpu.VMEM(y8.shape, f32),
             pltpu.VMEM(y8.shape, f32),
-            pltpu.SMEM((PEERS, 128), f32),
+            pltpu.VMEM((PEERS, 128), jnp.int32),
+            pltpu.SMEM((PEERS, 128), jnp.int32),
             pltpu.SemaphoreType.DMA((2,)),
             pltpu.SMEM((2 * PEERS * size + CAP + 3 * GROUP,), jnp.int32),
         ]
@@ -305,13 +326,13 @@
             owner = 2 * peer + half
             live = cnt[owner] - low
             for c in range(size):
-                block = jnp.where(c < live, ps[owner * CAP + low + c], SB)
+                block = jnp.where(c < live, ps[peer * (2 * CAP) + half * CAP + low + c], SB)
                 row = 3 * (half * size + c)
                 total = odd if (half * size + c) % 2 else even
                 total[block] = total[block] + force[peer, row : row + 3, :]
         return unused
 
-    lax.fori_loop(0, PEERS, one_peer, 0)
+    lax.fori_loop(0, PEERS, one_peer, 0, unroll=2)
     out[...] = even[0:SB] + odd[0:SB]
 
 
@@ -337,7 +358,7 @@
 def body(slave_coords, slave_weight, master_ctrl, master_wt, pair_slave, pair_master, pair_count):
     coords = slave_coords.reshape(3, SB, QP).transpose(1, 0, 2)
     payload = pack(
-        0, CAP, pair_slave, pair_master, pair_count, coords, slave_weight.reshape(SB, QP)
+        CAP, pair_slave, pair_master, pair_count, coords, slave_weight.reshape(SB, QP)
     )
     tiles = exchange(payload)
 

time: 107 us -> 104 us (0.972)
  Pallas kernels: 49 us -> 46.8 us
    pallas_call x1, Pallas kernels: 32.1 us -> 30.6 us  [forces(): pl.pallas_call(functools.partial(force_kernel, size), name='forces', out_...]
  transfers between devices with their start and end apart: 4 -> 4, of which waited for: 3 -> 3; matrix products, arithmetic and copies ran while one was open for 4% -> 4% of each run, Pallas kernels for 8% -> 9%
where the time goes in v4:
time: 104 us
  Pallas kernels  46.8 us (45%)
  waiting for transfers between devices  26.9 us (26%)
  starting transfers between devices  23.3 us (22%)
  local copies, waits for them, and re-layouts  4.33 us (4%)
  matrix products  1.75 us (2%)
    pallas_call x1, Pallas kernels, forces(): pl.pallas_call(functools.partial(force_kernel, size), name='forces', out_...  30.6 us
    all_to_all x2, waiting for transfers between devices, exchange(): lax.all_to_all(x, ('gx', 'g'), split_axis=0, concat_axis=0, tiled=True)  24.3 us
    all_to_all x2, starting transfers between devices, exchange(): lax.all_to_all(x, ('gx', 'g'), split_axis=0, concat_axis=0, tiled=True)  23.1 us
    pallas_call x1, Pallas kernels, sample_tiles(): pl.pallas_call(sample_kernel, name='samples', out_shape=(jax.ShapeDtypeSt...  8.87 us
    pallas_call x1, Pallas kernels, gather_forces(): pl.pallas_call(functools.partial(gather_kernel, low, size), name='gather'...  3.95 us
    unnamed x18, local copies, waits for them, and re-layouts  3.46 us
    pallas_call x1, Pallas kernels, pack(): pl.pallas_call(functools.partial(pack_kernel, size), name='pack', out_sha...  3.38 us
    ppermute x2, waiting for transfers between devices, swap(): return lax.ppermute(x, 'core', [(0, 1), (1, 0)])  2.65 us
  transfers between devices with their start and end apart: 4, of which 3 were waited for; matrix products, arithmetic and copies ran while one was open for 4% of the time, Pallas kernels for 9%

profile of v4, /device:TPU:0, one launch (start us, length us, event | category | flops | bytes accessed | tf_op | source)
XLA Modules:
  0.0 103.9 jit_solution(22108668469396777)
XLA Ops:
  0.6 3.4 %pack.1 = f32[64,11,4,128]{3,2,1,0:T(4,128)} custom-call(s32[640]{0:T(1024)} %ps.3, s32[640]{0:T(1024)} %pm.1, s32[128]{0:T(128)} %cnt.3, f32[512,3,128]{2,1,0:T(4,128)} %bitcast.19, f32[512,128]{1,0:T(8,128)} %bitcast.20), custom_call_target="tpu_custom_call" | custom-call | tf_op jit(solution)/shard_map/pack/pallas_call | solution.py:89
  4.0 0.0 copy-start.3
  4.0 0.0 copy-start.1
  4.0 11.7 %all-to-all-start = ((f32[64,11,4,128]{3,2,1,0:T(4,128)}), f32[64,11,4,128]{3,2,1,0:T(4,128)S(1)}, u32[]{:S(2)}, u32[]{:S(2)}) async-start(f32[64,11,4,128]{3,2,1,0:T(4,128)} %pack.1), calls=%async_computation | async-start | bytes 2883584 | tf_op jit(solution)/shard_map/all_to_all | solution.py:351
  15.7 0.0 copy-done.3
  15.7 0.8 concatenate.9
  16.5 0.0 copy-start.5
  16.5 0.0 copy-done.1
  16.5 0.2 bitcast_dynamic-update-slice_fusion
  16.7 0.8 copy-done.5
  17.5 0.0 copy-start
  17.5 0.1 collective-permute-start
  17.6 2.6 %collective-permute-done.other = f32[4,256,256]{2,1,0:T(8,128)S(1)} collective-permute-done((f32[4,256,256]{2,1,0:T(8,128)S(1)}, f32[4,256,256]{2,1,0:T(8,128)S(1)}, u32[]{:S(2)}, u32[]{:S(2)}) %collective-permute-start) | collective-permute-done | bytes 1048608 | tf_op jit(solution)/shard_map/ppermute | solution.py:355
  20.2 0.0 copy-done
  20.2 0.0 copy-start.2
  20.2 1.0 copy-done.2
  21.2 8.9 %samples.1 = (f32[2,4096,128]{2,1,0:T(8,128)}, f32[256,256]{1,0:T(8,128)}) custom-call(f32[4,256,256]{2,1,0:T(8,128)} %copy-done, f32[4,256,256]{2,1,0:T(8,128)} %copy-done.2, f32[256,256]{1,0:T(8,128)} %constant.6.clone.table), custom_call_target="tpu_custom_call" | custom-call | tf_op jit(solution)/shard_map/samples/pallas_call | solution.py:143
  30.1 8.4 %all-to-all-done.tiles = f32[64,11,4,128]{3,2,1,0:T(4,128)S(1)} async-done(((f32[64,11,4,128]{3,2,1,0:T(4,128)}), f32[64,11,4,128]{3,2,1,0:T(4,128)S(1)}, u32[]{:S(2)}, u32[]{:S(2)}) %all-to-all-start) | async-done | bytes 1441824 | tf_op jit(solution)/shard_map/all_to_all | solution.py:351
  38.5 30.6 %forces.1 = (f32[64,32,128]{2,1,0:T(8,128)}, f32[3,256,256]{2,1,0:T(8,128)}, f32[3,256,256]{2,1,0:T(8,128)}) custom-call(s32[1]{0:T(128)} %bitcast.core, f32[64,11,4,128]{3,2,1,0:T(4,128)S(1)} %all-to-all-done.tiles, f32[2,4096,128]{2,1,0:T(8,128)} %get-tuple-element.7.y8_hbm), custom_call_target="tpu_custom_call" | custom-call | tf_op jit(solution)/shard_map/forces/pallas_call | solution.py:298
  69.2 0.0 copy-start.4
  69.2 0.0 copy-start.6
  69.2 0.0 copy-start.7
  69.2 0.1 collective-permute-start.1
  69.3 11.5 %all-to-all-start.1 = ((f32[64,32,128]{2,1,0:T(8,128)}), f32[64,32,128]{2,1,0:T(8,128)S(1)}, u32[]{:S(2)}, u32[]{:S(2)}) async-start(f32[64,32,128]{2,1,0:T(8,128)} %get-tuple-element.8), calls=%async_computation.1 | async-start | bytes 2097152 | tf_op jit(solution)/shard_map/all_to_all | solution.py:351
  80.8 0.0 copy-done.4
  80.8 0.1 mul.10
  80.9 0.0 collective-permute-done.1
  80.9 0.0 copy-done.6
  80.9 0.0 copy-done.7
  80.9 1.8 %fusion = f32[1,3,256,256]{3,2,1,0:T(8,128)S(1)} fusion(f32[256,256,1]{1,0,2:T(8,128)} %constant.7, f32[3,256,256]{2,1,0:T(8,128)S(1)} %copy-done.6, f32[3,256,256]{2,1,0:T(8,128)S(1)} %collective-permute-done.1, f32[256,256]{1,0:T(8,128)S(1)} %mul.10, f32[256,256]{1,0:T(8,128)S(1)} %copy-done.7), kind=kOutput, calls=%fused_computation.1 | convolution fusion | flops 604569600 | bytes 3145728 | tf_op jit(solution)/shard_map/cbj,jk->cbk/dot_general | solution.py:380
  82.6 1.5 %copy.11 = f32[1,3,256,256]{3,1,2,0:T(4,128)} copy(f32[1,3,256,256]{3,2,1,0:T(8,128)S(1)} %fusion) | data formatting | bytes 1572864
  84.2 15.8 %all-to-all-done.1.force = f32[64,32,128]{2,1,0:T(8,128)S(1)} async-done(((f32[64,32,128]{2,1,0:T(8,128)}), f32[64,32,128]{2,1,0:T(8,128)S(1)}, u32[]{:S(2)}, u32[]{:S(2)}) %all-to-all-start.1) | async-done | bytes 1048608 | tf_op jit(solution)/shard_map/all_to_all | solution.py:351
  100.0 4.0 %gather.1 = f32[512,3,128]{2,1,0:T(4,128)} custom-call(s32[640]{0:T(1024)} %ps.3, s32[128]{0:T(128)} %cnt.3, f32[64,32,128]{2,1,0:T(8,128)S(1)} %all-to-all-done.1.force), custom_call_target="tpu_custom_call" | custom-call | tf_op jit(solution)/shard_map/gather/pallas_call | solution.py:340
  (1 shorter events, 0.0 us)
Async XLA Ops:
  4.0 11.7 %copy-start.3 = (f32[65536]{0:T(1024)S(1)}, f32[65536]{0:T(1024)}, u32[]{:S(2)}) copy-start(f32[65536]{0:T(1024)} %param.11) | copy-start | bytes 786436
  4.0 12.5 %copy-start.1 = (f32[3,65536]{1,0:T(4,128)S(1)}, f32[3,65536]{1,0:T(4,128)}, u32[]{:S(2)}) copy-start(f32[3,65536]{1,0:T(4,128)} %param.10) | copy-start | bytes 2359300
  4.0 34.5 %all-to-all-start = ((f32[64,11,4,128]{3,2,1,0:T(4,128)}), f32[64,11,4,128]{3,2,1,0:T(4,128)S(1)}, u32[]{:S(2)}, u32[]{:S(2)}) async-start(f32[64,11,4,128]{3,2,1,0:T(4,128)} %pack.1), calls=%async_computation | async-start | bytes 2883584 | tf_op jit(solution)/shard_map/all_to_all | solution.py:351
  16.5 0.9 copy-start.5
  17.5 2.8 %copy-start = (f32[4,256,256]{2,1,0:T(8,128)}, f32[4,256,256]{2,1,0:T(8,128)S(1)}, u32[]{:S(2)}) copy-start(f32[4,256,256]{2,1,0:T(8,128)S(1)} %constant_dynamic-update-slice_fusion.own) | copy-start | bytes 3145732
  17.5 2.7 %collective-permute-start = (f32[4,256,256]{2,1,0:T(8,128)S(1)}, f32[4,256,256]{2,1,0:T(8,128)S(1)}, u32[]{:S(2)}, u32[]{:S(2)}) collective-permute-start(f32[4,256,256]{2,1,0:T(8,128)S(1)} %constant_dynamic-update-slice_fusion.own), channel_id=1, source_target_pairs={{0,1},{1,0},{2,3},{3,2},{4,5},{5,4},{6,7},{7,6},{8,9},{9,8},{10,11... | collective-permute-start | bytes 3145736 | tf_op jit(solution)/shard_map/ppermute | solution.py:355
  20.2 1.0 copy-start.2
  69.2 11.6 %copy-start.4 = (f32[65536]{0:T(1024)S(1)}, f32[65536]{0:T(1024)}, u32[]{:S(2)}) copy-start(f32[65536]{0:T(1024)} %param.11) | copy-start | bytes 786436
  69.2 11.7 %copy-start.6 = (f32[3,256,256]{2,1,0:T(8,128)S(1)}, f32[3,256,256]{2,1,0:T(8,128)}, u32[]{:S(2)}) copy-start(f32[3,256,256]{2,1,0:T(8,128)} %get-tuple-element.9) | copy-start | bytes 2359300
  69.2 11.7 %copy-start.7 = (f32[256,256]{1,0:T(8,128)S(1)}, f32[256,256]{1,0:T(8,128)}, u32[]{:S(2)}) copy-start(f32[256,256]{1,0:T(8,128)} %get-tuple-element.11) | copy-start | bytes 786436
  69.2 11.7 %collective-permute-start.1 = (f32[3,256,256]{2,1,0:T(8,128)}, f32[3,256,256]{2,1,0:T(8,128)S(1)}, u32[]{:S(2)}, u32[]{:S(2)}) collective-permute-start(f32[3,256,256]{2,1,0:T(8,128)} %get-tuple-element.10), channel_id=1, source_target_pairs={{0,1},{1,0},{2,3},{3,2},{4,5},{5,4},{6,7},{7,6},{8,9},{9,8},{10,11... | collective-permute-start | bytes 2359304 | tf_op jit(solution)/shard_map/ppermute | solution.py:355
  69.3 30.7 %all-to-all-start.1 = ((f32[64,32,128]{2,1,0:T(8,128)}), f32[64,32,128]{2,1,0:T(8,128)S(1)}, u32[]{:S(2)}, u32[]{:S(2)}) async-start(f32[64,32,128]{2,1,0:T(8,128)} %get-tuple-element.8), calls=%async_computation.1 | async-start | bytes 2097152 | tf_op jit(solution)/shard_map/all_to_all | solution.py:351

commit v5 on v4

--- a/solution.py
+++ b/solution.py
@@ -17,7 +17,10 @@
 MB = 256
 MP = 256
 PEERS = 64
-GROUP = 8
+TRIP = 32
+LAG = 4
+RING = 8
+SPARE = TRIP + LAG
 
 f32 = jnp.float32
 bf16 = jnp.bfloat16
@@ -217,9 +220,9 @@
 
     total = lax.fori_loop(0, PEERS, list_peer, jnp.int32(0), unroll=2)
     last = entries[jnp.maximum(total - 1, 0)]
-    for k in range(3 * GROUP):
+    for k in range(SPARE):
         entries[total + k] = last | (1 << 20)
-    trips = (total + 2 * GROUP - 1) // (2 * GROUP)
+    trips = (total + TRIP - 1) // TRIP
 
     load_y8.wait()
 
@@ -227,41 +230,37 @@
         entry = entries[index]
         return (entry >> 4) & 63, entry & 15, (entry >> 10) & 511, entry >> 20
 
-    def stage_front(group, which):
-        for u in range(GROUP):
-            peer, c, block, extra = unpack(group * GROUP + u)
-            keep = (1 - extra).astype(f32)
-            base = (which * GROUP + u) * PIECES
-            at = pl.ds(pl.multiple_of(block * 8, 8), 8)
-            samples = jnp.concatenate([y8[0, at, :], y8[1, at, :]], axis=1)
-            values = front(tiles[peer, c], samples, keep)
-            for k in range(PIECES):
-                buffers[base + k][...] = values[k]
-
-    def stage_back(group, which):
-        for u in range(GROUP):
-            peer, c, block, _ = unpack(group * GROUP + u)
-            base = (which * GROUP + u) * PIECES
-            high, low, ax2, ax8, lead, lead8, xs, scale = [
-                buffers[base + k][...] for k in range(PIECES)
-            ]
-            q = dot(ax2, high, 1, 0)
-            f = dot(lead, high, 1, 1)
-            q = q[0:8] + q[8:16] + dot(ax8, low, 1, 0)[0:8] * (1.0 / LIFT)
-            f = f[0:8] + f[8:16] + dot(lead8, low, 1, 1)[0:8] * (1.0 / LIFT)
-            f = scale * (xs * f[3:4] - f)
-            force[peer, pl.ds(c * 3, 3), :] = f[0:3]
-            at = pl.ds(pl.multiple_of(block * 8, 8), 8)
-            for h in range(2):
-                acc[h, at, :] = acc[h, at, :] + q[:, 128 * h : 128 * h + 128]
-
-    stage_front(0, 0)
+    def stage_front(index, place):
+        peer, c, block, extra = unpack(index)
+        keep = (1 - extra).astype(f32)
+        at = pl.ds(pl.multiple_of(block * 8, 8), 8)
+        samples = jnp.concatenate([y8[0, at, :], y8[1, at, :]], axis=1)
+        values = front(tiles[peer, c], samples, keep)
+        for k in range(PIECES):
+            buffers[place * PIECES + k][...] = values[k]
+
+    def stage_back(index, place):
+        peer, c, block, _ = unpack(index)
+        high, low, ax2, ax8, lead, lead8, xs, scale = [
+            buffers[place * PIECES + k][...] for k in range(PIECES)
+        ]
+        q = dot(ax2, high, 1, 0)
+        f = dot(lead, high, 1, 1)
+        q = q[0:8] + q[8:16] + dot(ax8, low, 1, 0)[0:8] * (1.0 / LIFT)
+        f = f[0:8] + f[8:16] + dot(lead8, low, 1, 1)[0:8] * (1.0 / LIFT)
+        f = scale * (xs * f[3:4] - f)
+        force[peer, pl.ds(c * 3, 3), :] = f[0:3]
+        at = pl.ds(pl.multiple_of(block * 8, 8), 8)
+        for h in range(2):
+            acc[h, at, :] = acc[h, at, :] + q[:, 128 * h : 128 * h + 128]
+
+    for u in range(LAG):
+        stage_front(u, u)
 
     def trip(i, unused):
-        stage_front(2 * i + 1, 1)
-        stage_back(2 * i, 0)
-        stage_front(2 * i + 2, 0)
-        stage_back(2 * i + 1, 1)
+        for u in range(TRIP):
+            stage_front(i * TRIP + u + LAG, (u + LAG) % RING)
+            stage_back(i * TRIP + u, u % RING)
         return unused
 
     lax.fori_loop(0, trips, trip, 0)
@@ -307,9 +306,9 @@
             pltpu.VMEM((PEERS, 128), jnp.int32),
             pltpu.SMEM((PEERS, 128), jnp.int32),
             pltpu.SemaphoreType.DMA((2,)),
-            pltpu.SMEM((2 * PEERS * size + CAP + 3 * GROUP,), jnp.int32),
+            pltpu.SMEM((2 * PEERS * size + CAP + SPARE,), jnp.int32),
         ]
-        + one * (2 * GROUP),
+        + one * RING,
     )(core, tiles, y8)
 
 

time: 104 us -> 96.6 us (0.929)
  Pallas kernels: 46.8 us -> 40.4 us
  starting transfers between devices: 23.3 us -> 22 us
    pallas_call x1, Pallas kernels: 30.6 us -> 24.2 us  [forces(): pl.pallas_call(functools.partial(force_kernel, size), name='forces', out_...]
    all_to_all x2, starting transfers between devices: 23.1 us -> 21.8 us  [exchange(): lax.all_to_all(x, ('gx', 'g'), split_axis=0, concat_axis=0, tiled=True)]
where the time goes in v5:
time: 96.6 us; the launch traced here: 96.2 us
  Pallas kernels  40.4 us (42%)
  waiting for transfers between devices  26.9 us (28%)
  starting transfers between devices  22 us (23%)
  local copies, waits for them, and re-layouts  4.33 us (4%)
  matrix products  1.75 us (2%)
    all_to_all x2, waiting for transfers between devices, exchange(): lax.all_to_all(x, ('gx', 'g'), split_axis=0, concat_axis=0, tiled=True)  24.3 us
    pallas_call x1, Pallas kernels, forces(): pl.pallas_call(functools.partial(force_kernel, size), name='forces', out_...  24.2 us
    all_to_all x2, starting transfers between devices, exchange(): lax.all_to_all(x, ('gx', 'g'), split_axis=0, concat_axis=0, tiled=True)  21.8 us
    pallas_call x1, Pallas kernels, sample_tiles(): pl.pallas_call(sample_kernel, name='samples', out_shape=(jax.ShapeDtypeSt...  8.87 us
    pallas_call x1, Pallas kernels, gather_forces(): pl.pallas_call(functools.partial(gather_kernel, low, size), name='gather'...  3.95 us
    unnamed x18, local copies, waits for them, and re-layouts  3.46 us
    pallas_call x1, Pallas kernels, pack(): pl.pallas_call(functools.partial(pack_kernel, size), name='pack', out_sha...  3.38 us
    ppermute x2, waiting for transfers between devices, swap(): return lax.ppermute(x, 'core', [(0, 1), (1, 0)])  2.65 us
  transfers between devices with their start and end apart: 4, of which 3 were waited for; matrix products, arithmetic and copies ran while one was open for 4% of the time, Pallas kernels for 9%

profile of v5, /device:TPU:0, one launch (start us, length us, event | category | flops | bytes accessed | tf_op | source)
XLA Modules:
  0.0 96.2 jit_solution(1455789498848155695)
XLA Ops:
  0.6 3.4 %pack.1 = f32[64,11,4,128]{3,2,1,0:T(4,128)} custom-call(s32[640]{0:T(1024)} %ps.3, s32[640]{0:T(1024)} %pm.1, s32[128]{0:T(128)} %cnt.3, f32[512,3,128]{2,1,0:T(4,128)} %bitcast.19, f32[512,128]{1,0:T(8,128)} %bitcast.20), custom_call_target="tpu_custom_call" | custom-call | tf_op jit(solution)/shard_map/pack/pallas_call | solution.py:92
  4.0 0.0 copy-start.3
  4.0 0.0 copy-start.1
  4.0 11.7 %all-to-all-start = ((f32[64,11,4,128]{3,2,1,0:T(4,128)}), f32[64,11,4,128]{3,2,1,0:T(4,128)S(1)}, u32[]{:S(2)}, u32[]{:S(2)}) async-start(f32[64,11,4,128]{3,2,1,0:T(4,128)} %pack.1), calls=%async_computation | async-start | bytes 2883584 | tf_op jit(solution)/shard_map/all_to_all | solution.py:350
  15.7 0.0 copy-done.3
  15.7 0.8 concatenate.9
  16.5 0.0 copy-start.5
  16.5 0.0 copy-done.1
  16.5 0.2 bitcast_dynamic-update-slice_fusion
  16.7 0.8 copy-done.5
  17.5 0.0 copy-start
  17.5 0.1 collective-permute-start
  17.6 2.6 %collective-permute-done.other = f32[4,256,256]{2,1,0:T(8,128)S(1)} collective-permute-done((f32[4,256,256]{2,1,0:T(8,128)S(1)}, f32[4,256,256]{2,1,0:T(8,128)S(1)}, u32[]{:S(2)}, u32[]{:S(2)}) %collective-permute-start) | collective-permute-done | bytes 1048608 | tf_op jit(solution)/shard_map/ppermute | solution.py:354
  20.2 0.0 copy-done
  20.2 0.0 copy-start.2
  20.2 1.0 %copy-done.2 = f32[4,256,256]{2,1,0:T(8,128)} copy-done((f32[4,256,256]{2,1,0:T(8,128)}, f32[4,256,256]{2,1,0:T(8,128)S(1)}, u32[]{:S(2)}) %copy-start.2) | copy-done | bytes 1048600
  21.2 8.9 %samples.1 = (f32[2,4096,128]{2,1,0:T(8,128)}, f32[256,256]{1,0:T(8,128)}) custom-call(f32[4,256,256]{2,1,0:T(8,128)} %copy-done, f32[4,256,256]{2,1,0:T(8,128)} %copy-done.2, f32[256,256]{1,0:T(8,128)} %constant.6.clone.table), custom_call_target="tpu_custom_call" | custom-call | tf_op jit(solution)/shard_map/samples/pallas_call | solution.py:146
  30.1 8.4 %all-to-all-done.tiles = f32[64,11,4,128]{3,2,1,0:T(4,128)S(1)} async-done(((f32[64,11,4,128]{3,2,1,0:T(4,128)}), f32[64,11,4,128]{3,2,1,0:T(4,128)S(1)}, u32[]{:S(2)}, u32[]{:S(2)}) %all-to-all-start) | async-done | bytes 1441824 | tf_op jit(solution)/shard_map/all_to_all | solution.py:350
  38.5 24.2 %forces.1 = (f32[64,32,128]{2,1,0:T(8,128)}, f32[3,256,256]{2,1,0:T(8,128)}, f32[3,256,256]{2,1,0:T(8,128)}) custom-call(s32[1]{0:T(128)} %bitcast.core, f32[64,11,4,128]{3,2,1,0:T(4,128)S(1)} %all-to-all-done.tiles, f32[2,4096,128]{2,1,0:T(8,128)} %get-tuple-element.7.y8_hbm), custom_call_target="tpu_custom_call" | custom-call | tf_op jit(solution)/shard_map/forces/pallas_call | solution.py:297
  62.7 0.0 copy-start.4
  62.7 0.0 copy-start.6
  62.7 0.0 copy-start.7
  62.7 0.1 collective-permute-start.1
  62.8 10.2 %all-to-all-start.1 = ((f32[64,32,128]{2,1,0:T(8,128)}), f32[64,32,128]{2,1,0:T(8,128)S(1)}, u32[]{:S(2)}, u32[]{:S(2)}) async-start(f32[64,32,128]{2,1,0:T(8,128)} %get-tuple-element.8), calls=%async_computation.1 | async-start | bytes 2097152 | tf_op jit(solution)/shard_map/all_to_all | solution.py:350
  73.0 0.0 copy-done.4
  73.0 0.1 mul.10
  73.1 0.0 collective-permute-done.1
  73.1 0.0 copy-done.6
  73.1 0.0 copy-done.7
  73.1 1.7 %fusion = f32[1,3,256,256]{3,2,1,0:T(8,128)S(1)} fusion(f32[256,256,1]{1,0,2:T(8,128)} %constant.7, f32[3,256,256]{2,1,0:T(8,128)S(1)} %copy-done.6, f32[3,256,256]{2,1,0:T(8,128)S(1)} %collective-permute-done.1, f32[256,256]{1,0:T(8,128)S(1)} %mul.10, f32[256,256]{1,0:T(8,128)S(1)} %copy-done.7), kind=kOutput, calls=%fused_computation.1 | convolution fusion | flops 604569600 | bytes 3145728 | tf_op jit(solution)/shard_map/cbj,jk->cbk/dot_general | solution.py:379
  74.9 1.5 %copy.11 = f32[1,3,256,256]{3,1,2,0:T(4,128)} copy(f32[1,3,256,256]{3,2,1,0:T(8,128)S(1)} %fusion) | data formatting | bytes 1572864
  76.4 15.8 %all-to-all-done.1.force = f32[64,32,128]{2,1,0:T(8,128)S(1)} async-done(((f32[64,32,128]{2,1,0:T(8,128)}), f32[64,32,128]{2,1,0:T(8,128)S(1)}, u32[]{:S(2)}, u32[]{:S(2)}) %all-to-all-start.1) | async-done | bytes 1048608 | tf_op jit(solution)/shard_map/all_to_all | solution.py:350
  92.2 4.0 %gather.1 = f32[512,3,128]{2,1,0:T(4,128)} custom-call(s32[640]{0:T(1024)} %ps.3, s32[128]{0:T(128)} %cnt.3, f32[64,32,128]{2,1,0:T(8,128)S(1)} %all-to-all-done.1.force), custom_call_target="tpu_custom_call" | custom-call | tf_op jit(solution)/shard_map/gather/pallas_call | solution.py:339
  (1 shorter events, 0.0 us)
Async XLA Ops:
  4.0 11.7 %copy-start.3 = (f32[65536]{0:T(1024)S(1)}, f32[65536]{0:T(1024)}, u32[]{:S(2)}) copy-start(f32[65536]{0:T(1024)} %param.11) | copy-start | bytes 786436
  4.0 12.5 %copy-start.1 = (f32[3,65536]{1,0:T(4,128)S(1)}, f32[3,65536]{1,0:T(4,128)}, u32[]{:S(2)}) copy-start(f32[3,65536]{1,0:T(4,128)} %param.10) | copy-start | bytes 2359300
  4.0 34.5 %all-to-all-start = ((f32[64,11,4,128]{3,2,1,0:T(4,128)}), f32[64,11,4,128]{3,2,1,0:T(4,128)S(1)}, u32[]{:S(2)}, u32[]{:S(2)}) async-start(f32[64,11,4,128]{3,2,1,0:T(4,128)} %pack.1), calls=%async_computation | async-start | bytes 2883584 | tf_op jit(solution)/shard_map/all_to_all | solution.py:350
  16.5 0.9 copy-start.5
  17.5 2.8 %copy-start = (f32[4,256,256]{2,1,0:T(8,128)}, f32[4,256,256]{2,1,0:T(8,128)S(1)}, u32[]{:S(2)}) copy-start(f32[4,256,256]{2,1,0:T(8,128)S(1)} %constant_dynamic-update-slice_fusion.own) | copy-start | bytes 3145732
  17.5 2.7 %collective-permute-start = (f32[4,256,256]{2,1,0:T(8,128)S(1)}, f32[4,256,256]{2,1,0:T(8,128)S(1)}, u32[]{:S(2)}, u32[]{:S(2)}) collective-permute-start(f32[4,256,256]{2,1,0:T(8,128)S(1)} %constant_dynamic-update-slice_fusion.own), channel_id=1, source_target_pairs={{0,1},{1,0},{2,3},{3,2},{4,5},{5,4},{6,7},{7,6},{8,9},{9,8},{10,11... | collective-permute-start | bytes 3145736 | tf_op jit(solution)/shard_map/ppermute | solution.py:354
  20.2 1.0 %copy-start.2 = (f32[4,256,256]{2,1,0:T(8,128)}, f32[4,256,256]{2,1,0:T(8,128)S(1)}, u32[]{:S(2)}) copy-start(f32[4,256,256]{2,1,0:T(8,128)S(1)} %collective-permute-done.other) | copy-start | bytes 3145732
  62.7 10.3 %copy-start.4 = (f32[65536]{0:T(1024)S(1)}, f32[65536]{0:T(1024)}, u32[]{:S(2)}) copy-start(f32[65536]{0:T(1024)} %param.11) | copy-start | bytes 786436
  62.7 10.4 %copy-start.6 = (f32[3,256,256]{2,1,0:T(8,128)S(1)}, f32[3,256,256]{2,1,0:T(8,128)}, u32[]{:S(2)}) copy-start(f32[3,256,256]{2,1,0:T(8,128)} %get-tuple-element.9) | copy-start | bytes 2359300
  62.7 10.4 %copy-start.7 = (f32[256,256]{1,0:T(8,128)S(1)}, f32[256,256]{1,0:T(8,128)}, u32[]{:S(2)}) copy-start(f32[256,256]{1,0:T(8,128)} %get-tuple-element.11) | copy-start | bytes 786436
  62.7 10.4 %collective-permute-start.1 = (f32[3,256,256]{2,1,0:T(8,128)}, f32[3,256,256]{2,1,0:T(8,128)S(1)}, u32[]{:S(2)}, u32[]{:S(2)}) collective-permute-start(f32[3,256,256]{2,1,0:T(8,128)} %get-tuple-element.10), channel_id=1, source_target_pairs={{0,1},{1,0},{2,3},{3,2},{4,5},{5,4},{6,7},{7,6},{8,9},{9,8},{10,11... | collective-permute-start | bytes 2359304 | tf_op jit(solution)/shard_map/ppermute | solution.py:354
  62.8 29.4 %all-to-all-start.1 = ((f32[64,32,128]{2,1,0:T(8,128)}), f32[64,32,128]{2,1,0:T(8,128)S(1)}, u32[]{:S(2)}, u32[]{:S(2)}) async-start(f32[64,32,128]{2,1,0:T(8,128)} %get-tuple-element.8), calls=%async_computation.1 | async-start | bytes 2097152 | tf_op jit(solution)/shard_map/all_to_all | solution.py:350
